TPU v7x, 32 devices: a whole 2x2x4 slice. The times are simulated.
32 devices in a mesh: space: 16 (over z, y, x), coil: 2 (over core).
Axes of the slice: x: 2, y: 2, z: 4, core: 2. Of those that a mesh axis runs over, the one named last changes fastest.
Arguments:
- state: bfloat16 [32, 2, 1024, 768], P(None, None, 'space', 'coil'), may hold values from -6 to 6
- sens: float32 [2, 16, 2, 1024, 768], P(None, 'coil', None, 'space'), may hold values from -2 to 2
- kdata: float32 [2, 16, 2, 768, 1024], P(None, 'coil', None, 'space'), may hold values from -3 to 3
- mask: int32 [768, 1024], P('space'), may hold values 0 or 1
- inject: float32 [32, 2], replicated, may hold values from -4 to 4
- kernels: bfloat16 [4, 27, 16, 16], replicated, may hold values from -0.3125 to 0.3125
- biases: float32 [4, 16], replicated, may hold values from -3 to 3
- mixers: bfloat16 [4, 16, 16], replicated, may hold values from -1.5 to 1.5
Outputs:
- new_state: bfloat16 [32, 2, 1024, 768], P(None, None, 'space', 'coil')
- gradient: float32 [2, 2, 1024, 768], P(None, None, 'space', 'coil')
All inputs are finite; a program needn't handle non-finite values. No bound on the sum of `mask` on one device may be relied on, other than what follows from the above.
Results may differ from a plain program's by a relative error of at most 0.015.
Values may be sent and summed in bfloat16 or wider, within the bound.
A program may use at most 128 MiB of HBM per device.

v0:
```python
import math

import jax
import jax.numpy as jnp
from jax import lax
from jax.sharding import PartitionSpec as P


def padded_2(cells, sides, width):
    for axis, dim in sides:
        count = lax.axis_size(axis)
        ends = count - 1
        head = lax.slice_in_dim(cells, 0, width, axis=dim)
        tail = lax.slice_in_dim(cells, cells.shape[dim] - width, cells.shape[dim], axis=dim)
        cells = jnp.concatenate(
            [
                lax.ppermute(tail, axis, [(i, (i + 1) % count) for i in range(ends)]),
                cells,
                lax.ppermute(head, axis, [((i + 1) % count, i) for i in range(ends)]),
            ],
            axis=dim,
        )
    return cells


def dft_table(length):
    index = lax.iota(jnp.int32, length)
    product = index[:, None] * index[None, :] % length
    angle = product.astype(jnp.float32) * (2.0 * math.pi / length)
    scale = 1.0 / math.sqrt(length)
    return jnp.concatenate([jnp.cos(angle) * scale, jnp.sin(angle) * scale], axis=1)


def transform(stacked, table, length, sign, form):
    result = jnp.einsum(form, stacked, table, precision=lax.Precision.HIGHEST)
    real_cos = result[0, ..., :length]
    real_sin = result[0, ..., length:]
    imag_cos = result[1, ..., :length]
    imag_sin = result[1, ..., length:]
    return jnp.stack([real_cos - sign * imag_sin, imag_cos + sign * real_sin])


def convolve(padded, kernel, bias, mixer):
    weight = jnp.transpose(
        kernel.reshape(3, 3, 3, kernel.shape[1], kernel.shape[2]), (3, 4, 0, 1, 2)
    )
    raw = lax.conv_general_dilated(
        padded[None],
        weight,
        (1, 1, 1),
        ((1, 1), (0, 0), (0, 0)),
        dimension_numbers=("NCDHW", "OIDHW", "NCDHW"),
        preferred_element_type=jnp.float32,
    )[0]
    hidden = jax.nn.relu(raw + bias[:, None, None, None]).astype(jnp.bfloat16)
    return jnp.einsum("oi,ipqr->opqr", mixer, hidden, preferred_element_type=jnp.float32)


def per_device(state, sens, kdata, mask, inject, kernels, biases, mixers):
    npar = sens.shape[4]
    npe = kdata.shape[4]
    estimate = lax.all_gather(state[0:2], "coil", axis=3, tiled=True).astype(jnp.float32)
    coil_real = sens[0] * estimate[0][None] - sens[1] * estimate[1][None]
    coil_imag = sens[0] * estimate[1][None] + sens[1] * estimate[0][None]
    coil_images = jnp.stack([coil_real, coil_imag])
    par_table = dft_table(npar)
    pe_table = dft_table(npe)
    columns_done = transform(coil_images, par_table, npar, -1.0, "rcpqn,nk->rcpqk")
    spectra = lax.all_to_all(
        columns_done.astype(jnp.bfloat16), "space", split_axis=4, concat_axis=3, tiled=True
    ).astype(columns_done.dtype)
    full = transform(spectra, pe_table, npe, -1.0, "rcpnq,nk->rcpqk")
    sampled = mask.astype(jnp.float32)
    residual = sampled * (full - kdata)
    lines = transform(residual, pe_table, npe, 1.0, "rcpqk,kn->rcpqn")
    returned = lax.all_to_all(
        lines.astype(jnp.bfloat16), "space", split_axis=4, concat_axis=3, tiled=True
    ).astype(lines.dtype)
    images = transform(returned, par_table, npar, 1.0, "rcpkn,kq->rcpnq")
    part_real = jnp.sum(sens[0] * images[0] + sens[1] * images[1], axis=0)
    part_imag = jnp.sum(sens[0] * images[1] - sens[1] * images[0], axis=0)
    gradient = lax.psum_scatter(
        jnp.stack([part_real, part_imag]).astype(jnp.bfloat16),
        "coil",
        scatter_dimension=3,
        tiled=True,
    ).astype(jnp.float32)
    added = jnp.einsum("cg,gpqr->cpqr", inject, gradient, precision=lax.Precision.HIGHEST)
    merged = (state.astype(jnp.float32) + added).astype(jnp.bfloat16)
    half = merged.shape[0] // 2
    layers = kernels.shape[0]
    first = merged[:half]
    second = merged[half:]
    for layer in range(layers):
        source = first if layer % 2 == 0 else second
        padded = padded_2(source, (("space", 2), ("coil", 3)), 1)
        update = convolve(padded, kernels[layer], biases[layer], mixers[layer])
        if layer % 2 == 0:
            second = (second.astype(jnp.float32) + update).astype(jnp.bfloat16)
        else:
            first = (first.astype(jnp.float32) + update).astype(jnp.bfloat16)
    new_state = jnp.concatenate([first, second], axis=0)
    return (new_state, gradient)


def solution(mesh):
    return jax.shard_map(
        per_device,
        mesh=mesh,
        in_specs=(
            P(None, None, "space", "coil"),
            P(None, "coil", None, "space", None),
            P(None, "coil", None, "space", None),
            P("space", None),
            P(),
            P(),
            P(),
            P(),
        ),
        out_specs=(P(None, None, "space", "coil"), P(None, None, "space", "coil")),
        check_vma=False,
    )
```

profile of v0, /device:TPU:15, one launch (start us, length us, event | category | flops | bytes accessed | tf_op | source)
XLA Modules:
  0.0 895.1 jit_solution(10768876438203070891)
XLA Ops:
  21.5 32.6 %fusion.34 = f32[2,8,2,64,1536]{4,3,2,1,0:T(8,128)S(1)} fusion(f32[1,8,2,64,768]{4,3,2,1,0:T(8,128)S(1)} %get-tuple-element.19, f32[1,8,2,64,768]{4,3,2,1,0:T(8,128)S(1)} %get-tuple-element.18, f32[768,768]{1,0:T(8,128)S(1)} %get-tuple-element.46, f32[768,768]{1,0:T(8,128)} %get-tuple-element.47), kind=kOutput, calls=%fused_computation.37 | convolution fusion | flops 28993781760 | bytes 23592960 | tf_op jit(solution)/shard_map/rcpqn,nk->rcpqk/dot_general | solution.py:35
  66.7 12.7 %reshape.78 = bf16[16,2,49152]{2,1,0:T(2,128)(2,1)} reshape(bf16[768,2,8,2,64]{4,3,2,1,0:T(2,128)(2,1)} %bitcast.171) | data formatting | bytes 6291456
  86.2 17.8 %sine_multiply_fusion = (f32[1024,1024]{1,0:T(8,128)}, f32[1024,1024]{1,0:T(8,128)}) fusion(), kind=kLoop, calls=%fused_computation.55 | loop fusion | flops 16777216 | bytes 8388608 | tf_op jit(solution)/shard_map/mul | solution.py:31
  104.0 53.4 %all-to-all-done = bf16[16,2,49152]{2,1,0:T(2,128)(2,1)S(1)} async-done(((bf16[16,2,49152]{2,1,0:T(2,128)(2,1)}), bf16[16,2,49152]{2,1,0:T(2,128)(2,1)S(1)}, u32[]{:S(2)}, u32[]{:S(2)}) %all-to-all-start) | async-done | bytes 3145760 | tf_op jit(solution)/shard_map/all_to_all | solution.py:69
  183.7 23.3 %fusion.29 = f32[2,8,2,48,2048]{4,3,2,1,0:T(8,128)S(1)} fusion(bf16[2,8,2,1024,48]{3,4,2,1,0:T(8,128)(2,1)S(1)} %all_to_all.29, f32[1024,1024]{1,0:T(8,128)} %get-tuple-element.48, f32[1024,1024]{1,0:T(8,128)} %get-tuple-element.49), kind=kOutput, calls=%fused_computation.32 | convolution fusion | flops 38656802816 | bytes 24117248 | tf_op jit(solution)/shard_map/rcpnq,nk->rcpqk/dot_general | solution.py:35
  211.2 48.3 %fusion.28 = f32[2,8,2,48,2048]{4,3,2,1,0:T(8,128)S(1)} fusion(f32[1024,1024]{1,0:T(8,128)} %get-tuple-element.48, f32[1024,1024]{1,0:T(8,128)} %get-tuple-element.49, f32[2,8,2,48,1024]{4,3,2,1,0:T(8,128)} %param.10, f32[1,8,2,48,1024]{4,3,2,1,0:T(8,128)} %get-tuple-element.15, f32[1,8,2,48,1024]{4,3,2,1,0:T(8,128)} %get-tuple-element.14, ...), kind=kOutput, calls=%fused_computation.31 | convolution fusion | flops 38661521408 | bytes 33751040 | tf_op jit(solution)/shard_map/rcpqk,kn->rcpqn/dot_general | solution.py:35
  261.0 15.4 %copy.112 = bf16[2,8,2,48,1024]{3,2,1,0,4:T(2,128)(2,1)} copy(bf16[2,8,2,48,1024]{4,3,2,1,0:T(8,128)(2,1)S(1)} %pad_maximum_fusion.1) | data formatting | bytes 6291456 | tf_op jit(solution)/shard_map/stack | solution.py:40
  276.4 15.4 %reshape.80 = bf16[16,2,49152]{2,1,0:T(2,128)(2,1)S(1)} reshape(bf16[1024,2,8,2,48]{4,3,2,1,0:T(2,128)(2,1)} %bitcast.168) | data formatting | bytes 6291456
  291.8 73.3 %all_to_all.36 = bf16[16,2,49152]{2,1,0:T(2,128)(2,1)} all-to-all(bf16[16,2,49152]{2,1,0:T(2,128)(2,1)S(1)} %reshape.80), channel_id=1, replica_groups=mesh['space'=16,'coil'=2] {'space'}, dimensions={0} | all-to-all | bytes 6291456 | tf_op jit(solution)/shard_map/all_to_all | solution.py:76
  365.1 14.5 %reshape.81 = bf16[1024,2,8,2,48]{4,3,2,1,0:T(2,128)(2,1)} reshape(bf16[16,2,49152]{2,1,0:T(2,128)(2,1)} %all_to_all.36) | data formatting | bytes 6291456
  379.6 12.1 %copy.179 = bf16[2,8,2,48,16,64]{3,4,5,2,1,0:T(8,128)(2,1)} copy(bf16[2,8,2,48,16,64]{3,2,1,0,5,4:T(2,128)(2,1)} %bitcast.169) | data formatting | bytes 6291456 | tf_op jit(solution)/shard_map/all_to_all | solution.py:76
  391.6 12.8 %all_to_all.33 = bf16[2,8,2,768,64]{3,4,2,1,0:T(8,128)(2,1)} reshape(bf16[2,8,2,16,48,64]{4,3,5,2,1,0:T(8,128)(2,1)} %bitcast.170) | data formatting | bytes 6291456 | tf_op jit(solution)/shard_map/all_to_all | solution.py:76
  404.4 19.0 %fusion.49 = f32[2,8,2,64,1536]{4,3,2,1,0:T(8,128)S(1)} fusion(bf16[2,8,2,768,64]{3,4,2,1,0:T(8,128)(2,1)} %all_to_all.33, f32[768,768]{1,0:T(8,128)} %copy-done.9, f32[768,768]{1,0:T(8,128)} %get-tuple-element.47), kind=kOutput, calls=%fused_computation.60 | convolution fusion | flops 28992208896 | bytes 20447232 | tf_op jit(solution)/shard_map/rcpkn,kq->rcpnq/dot_general | solution.py:35
  490.8 36.8 %maximum_convert_fusion.3 = bf16[2,64,8,49,16]{4,2,3,1,0:T(8,128)(2,1)} fusion(bf16[3,3,3,16,16]{4,3,2,1,0:T(8,128)(2,1)S(1)} %bitcast.190, bf16[16,2,66,1,7,2]{0,4,5,2,1,3:T(8,128)(2,1)S(1)} %slice.244, bf16[16,2,66,1,8,49]{0,4,5,2,1,3:T(8,128)(2,1)} %copy.121, f32[16]{0:T(128)S(1)} %get-tuple-element.44, pred[8,49]{0,1:T(8,128)(4,1)S(1)} %copy-done.18), kind=kOutput, calls=%fused_computation.8 | convolution fusion | flops 470803456 | bytes 3334856 | tf_op jit(solution)/shard_map/conv_general_dilated | solution.py:47
  527.7 13.2 %copy.123 = bf16[2,64,8,49,16]{1,4,3,2,0:T(8,128)(2,1)S(1)} copy(bf16[2,64,8,49,16]{4,2,3,1,0:T(8,128)(2,1)} %maximum_convert_fusion.3) | data formatting | bytes 3211264 | tf_op jit(solution)/shard_map/convert_element_type | solution.py:55
  578.4 12.6 %copy.131 = bf16[16,2,66,1,8,49]{0,4,5,2,1,3:T(8,128)(2,1)} copy(bf16[16,2,66,1,8,49]{2,0,5,4,1,3:T(8,128)(2,1)} %bitcast.178) | data formatting | bytes 3311616 | tf_op jit(solution)/shard_map/conv_general_dilated | solution.py:47
  592.2 36.8 %maximum_convert_fusion.2 = bf16[2,64,8,49,16]{4,2,3,1,0:T(8,128)(2,1)} fusion(bf16[3,3,3,16,16]{4,3,2,1,0:T(8,128)(2,1)S(1)} %bitcast.191, bf16[16,2,66,1,7,2]{0,4,5,2,1,3:T(8,128)(2,1)S(1)} %slice.248, bf16[16,2,66,1,8,49]{0,4,5,2,1,3:T(8,128)(2,1)} %copy.131, f32[16]{0:T(128)S(1)} %get-tuple-element.43, pred[8,49]{0,1:T(8,128)(4,1)S(1)} %copy-done.18), kind=kOutput, calls=%fused_computation.7 | convolution fusion | flops 470803456 | bytes 3334856 | tf_op jit(solution)/shard_map/conv_general_dilated | solution.py:47
  629.1 14.1 %copy.133 = bf16[2,64,8,49,16]{1,4,3,2,0:T(8,128)(2,1)} copy(bf16[2,64,8,49,16]{4,2,3,1,0:T(8,128)(2,1)} %maximum_convert_fusion.2) | data formatting | bytes 3211264 | tf_op jit(solution)/shard_map/convert_element_type | solution.py:55
  689.8 12.6 %copy.141 = bf16[16,2,66,1,8,49]{0,4,5,2,1,3:T(8,128)(2,1)} copy(bf16[16,2,66,1,8,49]{2,0,5,4,1,3:T(8,128)(2,1)} %bitcast.179) | data formatting | bytes 3311616 | tf_op jit(solution)/shard_map/conv_general_dilated | solution.py:47
  703.6 36.8 %maximum_convert_fusion.1 = bf16[2,64,8,49,16]{4,2,3,1,0:T(8,128)(2,1)} fusion(bf16[3,3,3,16,16]{4,3,2,1,0:T(8,128)(2,1)S(1)} %bitcast.192, bf16[16,2,66,1,7,2]{0,4,5,2,1,3:T(8,128)(2,1)S(1)} %slice.252, bf16[16,2,66,1,8,49]{0,4,5,2,1,3:T(8,128)(2,1)} %copy.141, f32[16]{0:T(128)S(1)} %get-tuple-element.45, pred[8,49]{0,1:T(8,128)(4,1)S(1)} %copy-done.18), kind=kOutput, calls=%fused_computation.6 | convolution fusion | flops 470803456 | bytes 3334856 | tf_op jit(solution)/shard_map/conv_general_dilated | solution.py:47
  740.4 13.8 %copy.143 = bf16[2,64,8,49,16]{1,4,3,2,0:T(8,128)(2,1)} copy(bf16[2,64,8,49,16]{4,2,3,1,0:T(8,128)(2,1)} %maximum_convert_fusion.1) | data formatting | bytes 3211264 | tf_op jit(solution)/shard_map/convert_element_type | solution.py:55
  808.4 12.6 %copy.151 = bf16[16,2,66,1,8,49]{0,4,5,2,1,3:T(8,128)(2,1)} copy(bf16[16,2,66,1,8,49]{2,0,5,4,1,3:T(8,128)(2,1)} %bitcast.176) | data formatting | bytes 3311616 | tf_op jit(solution)/shard_map/conv_general_dilated | solution.py:47
  822.3 37.0 %maximum_convert_fusion = bf16[2,64,8,49,16]{4,2,3,1,0:T(8,128)(2,1)} fusion(bf16[3,3,3,16,16]{4,3,2,1,0:T(8,128)(2,1)S(1)} %bitcast.189, bf16[16,2,66,1,7,2]{0,4,5,2,1,3:T(8,128)(2,1)S(1)} %slice.256, bf16[16,2,66,1,8,49]{0,4,5,2,1,3:T(8,128)(2,1)} %copy.151, f32[16]{0:T(128)S(1)} %copy-done.17, pred[8,49]{0,1:T(8,128)(4,1)S(1)} %copy-done.19), kind=kOutput, calls=%fused_computation.5 | convolution fusion | flops 470803456 | bytes 3334856 | tf_op jit(solution)/shard_map/conv_general_dilated | solution.py:47
  859.3 13.7 %copy.153 = bf16[2,64,8,49,16]{1,4,3,2,0:T(8,128)(2,1)} copy(bf16[2,64,8,49,16]{4,2,3,1,0:T(8,128)(2,1)} %maximum_convert_fusion) | data formatting | bytes 3211264 | tf_op jit(solution)/shard_map/convert_element_type | solution.py:55
  (169 shorter events, 289.4 us)
Async XLA Ops:
  7.2 435.7 %copy-start = (f32[32,2]{0,1:T(2,128)S(1)}, f32[32,2]{0,1:T(2,128)}, u32[]{:S(2)}) copy-start(f32[32,2]{0,1:T(2,128)} %param.12) | copy-start | bytes 772
  79.4 78.0 %all-to-all-start = ((bf16[16,2,49152]{2,1,0:T(2,128)(2,1)}), bf16[16,2,49152]{2,1,0:T(2,128)(2,1)S(1)}, u32[]{:S(2)}, u32[]{:S(2)}) async-start(bf16[16,2,49152]{2,1,0:T(2,128)(2,1)} %reshape.78), calls=%async_computation | async-start | bytes 6291456 | tf_op jit(solution)/shard_map/all_to_all | solution.py:69
  86.1 354.2 %reduce-scatter.4.cloned.1.call-start = ((), (), s32[]{:S(2)}) async-start(), calls=%async_computation.3 | async-start | bytes 589824
  391.6 31.8 %slice-start = ((s8[6291456]{0:T(1024)(128)(4,1)}), s8[2097152]{0:T(1024)(128)(4,1)S(1)}, s32[]{:S(2)}) async-start(s8[6291456]{0:T(1024)(128)(4,1)} %bitcast.174), calls=%async_computation.4 | async-start | bytes 4194304
  404.4 19.0 %slice-start.1 = ((s8[6291456]{0:T(1024)(128)(4,1)}), s8[4194304]{0:T(1024)(128)(4,1)S(1)}, s32[]{:S(2)}) async-start(s8[6291456]{0:T(1024)(128)(4,1)} %bitcast.174), calls=%async_computation.5 | async-start | bytes 8388608
  425.6 17.3 %copy-start.6 = (bf16[32,2,64,384]{3,2,1,0:T(8,128)(2,1)S(1)}, bf16[32,2,64,384]{3,2,1,0:T(8,128)(2,1)}, u32[]{:S(2)}) copy-start(bf16[32,2,64,384]{3,2,1,0:T(8,128)(2,1)} %param.8) | copy-start | bytes 9437188
  448.9 6.1 collective-permute-start
  452.0 6.4 collective-permute-start.1
  459.2 6.1 collective-permute-start.2
  461.0 4.8 collective-permute-start.3
  549.9 5.3 collective-permute-start.4
  551.8 6.4 collective-permute-start.5
  559.0 5.1 collective-permute-start.6
  560.8 3.8 collective-permute-start.7
  655.3 5.3 collective-permute-start.8
  657.3 6.4 collective-permute-start.9
  666.4 6.5 collective-permute-start.10
  669.2 5.0 collective-permute-start.11
  766.0 21.3 %copy-start.8 = (bf16[384,2,2,64]{3,2,1,0:T(2,128)(2,1)S(1)}, bf16[384,2,2,64]{3,2,1,0:T(2,128)(2,1)}, u32[]{:S(2)}) copy-start(bf16[384,2,2,64]{3,2,1,0:T(2,128)(2,1)} %copy-done.7) | copy-start | bytes 589828
  766.0 5.4 collective-permute-start.12
  768.1 6.4 collective-permute-start.13
  776.3 17.9 %copy-start.3 = (bf16[16,2,64,384]{3,0,2,1:T(8,128)(2,1)S(1)}, bf16[16,2,64,384]{3,0,2,1:T(8,128)(2,1)}, u32[]{:S(2)}) copy-start(bf16[16,2,64,384]{3,0,2,1:T(8,128)(2,1)} %copy-done.2) | copy-start | bytes 4718596
  778.0 12.2 %collective-permute-start.14 = (bf16[16,2,66,1]{2,0,3,1:T(8,128)(2,1)S(1)}, bf16[16,2,66,1]{2,0,3,1:T(8,128)(2,1)}, u32[]{:S(2)}, u32[]{:S(2)}) collective-permute-start(bf16[16,2,66,1]{2,0,3,1:T(8,128)(2,1)S(1)} %copy.145), channel_id=1, source_target_pairs={{0,1},{2,3},{4,5},{6,7},{8,9},{10,11},{12,13},{14,15},{16,17},{18,... | collective-permute-start | bytes 12680 | tf_op jit(solution)/shard_map/ppermute | solution.py:17
  781.4 10.8 %collective-permute-start.15 = (bf16[16,2,66,1]{2,0,3,1:T(8,128)(2,1)}, bf16[16,2,66,1]{2,0,3,1:T(8,128)(2,1)}, u32[]{:S(2)}, u32[]{:S(2)}) collective-permute-start(bf16[16,2,66,1]{2,0,3,1:T(8,128)(2,1)} %copy.146), channel_id=1, source_target_pairs={{1,0},{3,2},{5,4},{7,6},{9,8},{11,10},{13,12},{15,14},{17,16},{19,... | collective-permute-start | bytes 12680 | tf_op jit(solution)/shard_map/ppermute | solution.py:19
  (17 other events, 146.3 us)
Sparse Core Ops, SparseCore 0:
  430.6 9.6 reduce-scatter.3
where the time goes:
time: 913 us; the launch traced here: 895 us
  local copies, waits for them, and re-layouts  338 us (37%)
  matrix products  285 us (31%)
  blocking collectives  75.7 us (8%)
  waiting for transfers between devices  75.7 us (8%)
  other arithmetic  58.7 us (6%)
  starting transfers between devices  47.3 us (5%)
  between operations  15.1 us (2%)
    conv_general_dilated x4, matrix products, convolve(): lax.conv_general_dilated(padded[None], weight, (1, 1, 1), ((1, 1), (0, 0)...  148 us
    dot_general x4, matrix products, transform(): result = jnp.einsum(form, stacked, table, precision=lax.Precision.HIGHEST)  123 us
    unnamed x61, local copies, waits for them, and re-layouts  107 us
    all_to_all x1, blocking collectives, per_device(): lax.all_to_all(lines.astype(jnp.bfloat16), 'space', split_axis=4, concat_...  73.3 us
    convert_element_type x8, local copies, waits for them, and re-layouts, convolve(): hidden = jax.nn.relu(raw + bias[:, None, None, None]).astype(jnp.bfloat16)  69.2 us
    conv_general_dilated x8, local copies, waits for them, and re-layouts, convolve(): lax.conv_general_dilated(padded[None], weight, (1, 1, 1), ((1, 1), (0, 0)...  53.9 us
    all_to_all x1, waiting for transfers between devices, per_device(): lax.all_to_all(columns_done.astype(jnp.bfloat16), 'space', split_axis=4,...  53.4 us
    mul x2, other arithmetic, dft_table(): jnp.sin(angle) * scale  28.4 us
  transfers between devices with their start and end apart: 18, of which 7 were waited for; matrix products, arithmetic and copies ran while one was open for 4% of the time, Pallas kernels for 0%

commit v1 on v0

v1 whole, which is shorter than its diff:
```python
import functools
import math

import jax
import jax.numpy as jnp
from jax import lax
from jax.experimental import pallas as pl
from jax.experimental.pallas import tpu as pltpu
from jax.sharding import PartitionSpec as P


def dft_table(length):
    index = lax.iota(jnp.int32, length)
    product = index[:, None] * index[None, :] % length
    angle = product.astype(jnp.float32) * (2.0 * math.pi / length)
    scale = 1.0 / math.sqrt(length)
    return jnp.concatenate([jnp.cos(angle) * scale, jnp.sin(angle) * scale], axis=1).astype(jnp.bfloat16)


def transform(stacked, table, length, sign, form):
    result = jnp.einsum(form, stacked.astype(jnp.bfloat16), table, preferred_element_type=jnp.float32)
    real_cos = result[0, ..., :length]
    real_sin = result[0, ..., length:]
    imag_cos = result[1, ..., :length]
    imag_sin = result[1, ..., length:]
    return jnp.stack([real_cos - sign * imag_sin, imag_cos + sign * real_sin])


HALO = 4
BLOCK = 6


def coupling_weights(kernels):
    layers, _, outs, ins = kernels.shape
    taps = kernels.reshape(layers, 3, 3, 3, outs, ins)
    rows = []
    for out_pos in range(2):
        rows.append(jnp.concatenate([taps[:, in_pos - out_pos + 1] for in_pos in range(2)], axis=-1))
    mixed = jnp.concatenate(rows, axis=-2)
    strip = jnp.concatenate([mixed[:, b] for b in range(3)], axis=-1)
    unit = 2 * ins
    bands = [
        jnp.pad(strip, ((0, 0), (0, 0), (0, 0), (unit * x, unit * (BLOCK - 1 - x)))) for x in range(BLOCK)
    ]
    return jnp.concatenate(bands, axis=-2)


def mixer_weights(mixers):
    layers, outs, ins = mixers.shape
    times = 2 * BLOCK
    eye = jnp.eye(times, dtype=mixers.dtype)
    spread = mixers[:, None, :, None, :] * eye[None, :, None, :, None]
    return spread.reshape(layers, times * outs, times * ins)


def couplings_body(layers, rows, width, lanes, total_rows, total_cols, unit,
                   place_ref, cells_ref, weight_ref, mixer_ref, bias_ref, out_ref, halves, shifted):
    halo_rows = rows + 2 * HALO
    row_start = place_ref[0] - HALO
    col_start = place_ref[1]
    lane = lax.broadcasted_iota(jnp.int32, (1, lanes), 1)
    column = jnp.where(lane >= lanes - HALO, lane - lanes, lane) + col_start
    column_ok = jnp.where((column >= 0) & (column < total_cols), 1.0, 0.0)
    for half in range(2):
        halves[half, 0:halo_rows * unit, :] = cells_ref[half]
        halves[half, halo_rows * unit:, :] = jnp.zeros(
            (halves.shape[1] - halo_rows * unit, lanes), halves.dtype)
        for side in range(2):
            shifted[2 * side, halo_rows * unit:, :] = jnp.zeros(
                (halves.shape[1] - halo_rows * unit, lanes), halves.dtype)
    for layer in range(layers):
        source, target = layer % 2, 1 - layer % 2

        def spread(index, _, source=source):
            at = pl.ds(pl.multiple_of(index * unit, unit), unit)
            line = halves[source, at, :].astype(jnp.float32)
            shifted[0, at, :] = pltpu.roll(line, 1, 1).astype(jnp.bfloat16)
            shifted[1, at, :] = halves[source, at, :]
            shifted[2, at, :] = pltpu.roll(line, lanes - 1, 1).astype(jnp.bfloat16)
            return 0

        lax.fori_loop(0, halves.shape[1] // unit, spread, 0)
        left = halo_rows - 2 * layer - 2
        steps = -(-left // BLOCK)

        def block(index, _, layer=layer, target=target):
            start = layer + index * BLOCK
            inside = pl.ds(pl.multiple_of(start * unit, unit), (BLOCK + 2) * unit)
            raw = jnp.dot(weight_ref[layer, 0], shifted[0, inside, :], preferred_element_type=jnp.float32)
            raw += jnp.dot(weight_ref[layer, 1], shifted[1, inside, :], preferred_element_type=jnp.float32)
            raw += jnp.dot(weight_ref[layer, 2], shifted[2, inside, :], preferred_element_type=jnp.float32)
            hidden = jnp.maximum(raw + bias_ref[layer], 0.0)
            step = lax.broadcasted_iota(jnp.int32, (BLOCK * unit, 1), 0) // unit
            row = step + (start + 1 + row_start)
            row_ok = jnp.where((row >= 0) & (row < total_rows), 1.0, 0.0)
            hidden = (hidden * row_ok * column_ok).astype(jnp.bfloat16)
            update = jnp.dot(mixer_ref[layer], hidden, preferred_element_type=jnp.float32)
            at = pl.ds(pl.multiple_of((start + 1) * unit, unit), BLOCK * unit)
            halves[target, at, :] = (halves[target, at, :].astype(jnp.float32) + update).astype(jnp.bfloat16)
            return 0

        lax.fori_loop(0, steps, block, 0)
    for half in range(2):
        out_ref[half] = halves[half, HALO * unit:(HALO + rows) * unit, 0:width]


def couple(merged, kernels, biases, mixers, total_rows, total_cols):
    channels, positions, rows, width = merged.shape
    half = channels // 2
    layers = kernels.shape[0]
    unit = half * positions
    lanes = -(-(width + 2 * HALO) // 128) * 128
    cells = jnp.transpose(merged.reshape(2, half, positions, rows, width), (0, 3, 2, 1, 4))
    cells = cells.reshape(2, rows, unit, width)
    count = lax.axis_size("coil")
    up = [(i, i + 1) for i in range(count - 1)]
    down = [(i + 1, i) for i in range(count - 1)]
    before = lax.ppermute(cells[..., width - HALO:], "coil", up)
    after = lax.ppermute(cells[..., :HALO], "coil", down)
    gap = jnp.zeros(cells.shape[:-1] + (lanes - width - 2 * HALO,), cells.dtype)
    cells = jnp.concatenate([cells, after, gap, before], axis=-1)
    count = lax.axis_size("space")
    up = [(i, i + 1) for i in range(count - 1)]
    down = [(i + 1, i) for i in range(count - 1)]
    above = lax.ppermute(cells[:, rows - HALO:], "space", up)
    below = lax.ppermute(cells[:, :HALO], "space", down)
    cells = jnp.concatenate([above, cells, below], axis=1)
    halo_rows = rows + 2 * HALO
    held = halo_rows + 8
    cells = cells.reshape(2, halo_rows * unit, lanes)
    place = jnp.stack([lax.axis_index("space") * rows, lax.axis_index("coil") * width]).astype(jnp.int32)
    bias = jnp.tile(biases, (1, positions * BLOCK))[:, :, None]
    vmem = pl.BlockSpec(memory_space=pltpu.VMEM)
    out = pl.pallas_call(
        functools.partial(couplings_body, layers, rows, width, lanes, total_rows, total_cols, unit),
        out_shape=jax.ShapeDtypeStruct((2, rows * unit, width), jnp.bfloat16),
        in_specs=[pl.BlockSpec(memory_space=pltpu.SMEM)] + [vmem] * 4,
        out_specs=vmem,
        scratch_shapes=[
            pltpu.VMEM((2, held * unit, lanes), jnp.bfloat16),
            pltpu.VMEM((3, held * unit, lanes), jnp.bfloat16),
        ],
        compiler_params=pltpu.CompilerParams(vmem_limit_bytes=56 * 1024 * 1024),
    )(place, cells, coupling_weights(kernels), mixer_weights(mixers), bias)
    out = out.reshape(2, rows, positions, half, width)
    return jnp.transpose(out, (0, 3, 2, 1, 4)).reshape(channels, positions, rows, width)


def per_device(state, sens, kdata, mask, inject, kernels, biases, mixers):
    npar = sens.shape[4]
    npe = kdata.shape[4]
    estimate = lax.all_gather(state[0:2], "coil", axis=3, tiled=True).astype(jnp.float32)
    coil_real = sens[0] * estimate[0][None] - sens[1] * estimate[1][None]
    coil_imag = sens[0] * estimate[1][None] + sens[1] * estimate[0][None]
    coil_images = jnp.stack([coil_real, coil_imag])
    par_table = dft_table(npar)
    pe_table = dft_table(npe)
    columns_done = transform(coil_images, par_table, npar, -1.0, "rcpqn,nk->rcpqk")
    spectra = lax.all_to_all(
        columns_done.astype(jnp.bfloat16), "space", split_axis=4, concat_axis=3, tiled=True
    ).astype(columns_done.dtype)
    full = transform(spectra, pe_table, npe, -1.0, "rcpnq,nk->rcpqk")
    sampled = mask.astype(jnp.float32)
    residual = sampled * (full - kdata)
    lines = transform(residual, pe_table, npe, 1.0, "rcpqk,kn->rcpqn")
    returned = lax.all_to_all(
        lines.astype(jnp.bfloat16), "space", split_axis=4, concat_axis=3, tiled=True
    ).astype(lines.dtype)
    images = transform(returned, par_table, npar, 1.0, "rcpkn,kq->rcpnq")
    part_real = jnp.sum(sens[0] * images[0] + sens[1] * images[1], axis=0)
    part_imag = jnp.sum(sens[0] * images[1] - sens[1] * images[0], axis=0)
    gradient = lax.psum_scatter(
        jnp.stack([part_real, part_imag]).astype(jnp.bfloat16),
        "coil",
        scatter_dimension=3,
        tiled=True,
    ).astype(jnp.float32)
    added = jnp.einsum("cg,gpqr->cpqr", inject, gradient, precision=lax.Precision.HIGHEST)
    merged = (state.astype(jnp.float32) + added).astype(jnp.bfloat16)
    new_state = couple(merged, kernels, biases, mixers, npe, npar)
    return (new_state, gradient)


def solution(mesh):
    return jax.shard_map(
        per_device,
        mesh=mesh,
        in_specs=(
            P(None, None, "space", "coil"),
            P(None, "coil", None, "space", None),
            P(None, "coil", None, "space", None),
            P("space", None),
            P(),
            P(),
            P(),
            P(),
        ),
        out_specs=(P(None, None, "space", "coil"), P(None, None, "space", "coil")),
        check_vma=False,
    )
```

time: 913 us -> 562 us (0.62)
  matrix products: 285 us -> 39.3 us
  local copies, waits for them, and re-layouts: 338 us -> 228 us
  blocking collectives: 75.7 us -> 2.39 us
  Pallas kernels: 0 us -> 57.8 us
  waiting for transfers between devices: 75.7 us -> 125 us
  starting transfers between devices: 47.3 us -> 20.4 us
    conv_general_dilated x4 -> x0, matrix products: 148 us -> none  [convolve(): lax.conv_general_dilated(padded[None], weight, (1, 1, 1), ((1, 1), (0, 0)...]
    dot_general x8 -> x4, matrix products: 132 us -> 32.7 us  [transform(): jnp.einsum(form, stacked.astype(jnp.bfloat16), table, preferred_element_t...]
    all_to_all x1 -> x0, blocking collectives: 73.3 us -> none  [per_device(): lax.all_to_all(lines.astype(jnp.bfloat16), 'space', split_axis=4, concat_...]
    convert_element_type x8 -> x0, local copies, waits for them, and re-layouts: 69.2 us -> none  [convolve(): hidden = jax.nn.relu(raw + bias[:, None, None, None]).astype(jnp.bfloat16)]
    all_to_all x0 -> x1, waiting for transfers between devices: none -> 66.9 us  [per_device(): lax.all_to_all(lines.astype(jnp.bfloat16), 'space', split_axis=4, concat_...]
    pallas_call x0 -> x1, Pallas kernels: none -> 57.8 us  [couple(): pl.pallas_call(functools.partial(couplings_body, layers, rows, width, lan...]
    conv_general_dilated x8 -> x0, local copies, waits for them, and re-layouts: 53.9 us -> none  [convolve(): lax.conv_general_dilated(padded[None], weight, (1, 1, 1), ((1, 1), (0, 0)...]
    unnamed x61 -> x45, local copies, waits for them, and re-layouts: 107 us -> 58.1 us
  transfers between devices with their start and end apart: 18 -> 7, of which waited for: 7 -> 4; matrix products, arithmetic and copies ran while one was open for 4% -> 12% of each run, Pallas kernels for 0% -> 0%
where the time goes in v1:
time: 562 us; the launch traced here: 551 us
  local copies, waits for them, and re-layouts  228 us (41%)
  waiting for transfers between devices  125 us (22%)
  other arithmetic  63.1 us (11%)
  Pallas kernels  57.8 us (10%)
  matrix products  39.3 us (7%)
  starting transfers between devices  20.4 us (4%)
  between operations  14.6 us (3%)
    all_to_all x1, waiting for transfers between devices, per_device(): lax.all_to_all(lines.astype(jnp.bfloat16), 'space', split_axis=4, concat_...  66.9 us
    unnamed x45, local copies, waits for them, and re-layouts  58.1 us
    pallas_call x1, Pallas kernels, couple(): pl.pallas_call(functools.partial(couplings_body, layers, rows, width, lan...  57.8 us
    all_to_all x1, waiting for transfers between devices, per_device(): lax.all_to_all(columns_done.astype(jnp.bfloat16), 'space', split_axis=4,...  53.1 us
    another operation x5, other arithmetic  34 us
    dot_general x4, matrix products, transform(): jnp.einsum(form, stacked.astype(jnp.bfloat16), table, preferred_element_t...  32.7 us
    another operation x2, local copies, waits for them, and re-layouts, transform(): return jnp.stack([real_cos - sign * imag_sin, imag_cos + sign * real_sin])  26.7 us
    all_to_all x2, local copies, waits for them, and re-layouts, per_device(): lax.all_to_all(lines.astype(jnp.bfloat16), 'space', split_axis=4, concat_...  24.8 us
  transfers between devices with their start and end apart: 7, of which 4 were waited for; matrix products, arithmetic and copies ran while one was open for 12% of the time, Pallas kernels for 0%

profile of v1, /device:TPU:15, one launch (start us, length us, event | category | flops | bytes accessed | tf_op | source)
XLA Modules:
  0.0 551.1 jit_solution(18170584806264283382)
XLA Ops:
  7.2 10.0 %multiply_convert_fusion.2 = (bf16[768,768]{1,0:T(8,128)(2,1)S(1)}, bf16[768,768]{1,0:T(8,128)(2,1)S(1)}) fusion(), kind=kLoop, calls=%fused_computation.54 | loop fusion | flops 7667712 | bytes 2359296 | tf_op jit(solution)/shard_map/convert.11
  31.2 11.5 %copy.43 = bf16[2,8,2,64,768]{3,2,1,0,4:T(2,128)(2,1)} copy(bf16[2,8,2,64,768]{4,3,2,1,0:T(8,128)(2,1)S(1)} %pad_maximum_fusion.2) | data formatting | bytes 6291456 | tf_op jit(solution)/shard_map/stack | solution.py:26
  42.6 12.7 %reshape.60 = bf16[16,2,49152]{2,1,0:T(2,128)(2,1)} reshape(bf16[768,2,8,2,64]{4,3,2,1,0:T(2,128)(2,1)} %bitcast.88) | data formatting | bytes 6291456
  62.4 18.0 %multiply_convert_fusion = (bf16[1024,1024]{1,0:T(8,128)(2,1)}, bf16[1024,1024]{1,0:T(8,128)(2,1)}) fusion(), kind=kLoop, calls=%fused_computation.16 | loop fusion | flops 18874368 | bytes 4194304 | tf_op jit(solution)/shard_map/convert.7
  80.3 53.1 %all-to-all-done = bf16[16,2,49152]{2,1,0:T(2,128)(2,1)S(1)} async-done(((bf16[16,2,49152]{2,1,0:T(2,128)(2,1)}), bf16[16,2,49152]{2,1,0:T(2,128)(2,1)S(1)}, u32[]{:S(2)}, u32[]{:S(2)}) %all-to-all-start) | async-done | bytes 3145760 | tf_op jit(solution)/shard_map/all_to_all | solution.py:159
  133.5 8.6 %reshape.61 = bf16[768,2,8,2,64]{4,3,2,1,0:T(2,128)(2,1)} reshape(bf16[16,2,49152]{2,1,0:T(2,128)(2,1)S(1)} %all-to-all-done) | data formatting | bytes 6291456
  142.1 9.5 %copy.79 = bf16[2,8,2,64,16,48]{3,4,5,2,1,0:T(8,128)(2,1)} copy(bf16[2,8,2,64,16,48]{3,2,1,0,5,4:T(2,128)(2,1)} %bitcast.89) | data formatting | bytes 6291456 | tf_op jit(solution)/shard_map/all_to_all | solution.py:159
  151.5 8.1 %all_to_all.29 = bf16[2,8,2,1024,48]{3,4,2,1,0:T(8,128)(2,1)S(1)} reshape(bf16[2,8,2,16,64,48]{4,3,5,2,1,0:T(8,128)(2,1)} %bitcast.90) | data formatting | bytes 6291456 | tf_op jit(solution)/shard_map/all_to_all | solution.py:159
  159.7 8.9 %fusion.24 = f32[2,8,2,48,2048]{4,3,2,1,0:T(8,128)S(1)} fusion(bf16[2,8,2,1024,48]{3,4,2,1,0:T(8,128)(2,1)S(1)} %all_to_all.29, bf16[1024,1024]{1,0:T(8,128)(2,1)} %get-tuple-element.26, bf16[1024,1024]{1,0:T(8,128)(2,1)} %get-tuple-element.27), kind=kOutput, calls=%fused_computation.50 | convolution fusion | flops 6450839552 | bytes 19922944 | tf_op jit(solution)/shard_map/rcpnq,nk->rcpqk/dot_general | solution.py:21
  170.8 11.3 %fusion.9 = f32[2,8,2,48,2048]{4,3,2,1,0:T(8,128)S(1)} fusion(f32[2,8,2,48,1024]{4,3,2,1,0:T(8,128)} %param.10, f32[1,8,2,48,1024]{4,3,2,1,0:T(8,128)S(1)} %get-tuple-element.7, f32[1,8,2,48,1024]{4,3,2,1,0:T(8,128)S(1)} %get-tuple-element.6, f32[48,1024]{1,0:T(8,128)S(1)} %convert_element_type.58, bf16[1024,1024]{1,0:T(8,128)(2,1)} %get-tuple-element.26, ...), kind=kOutput, calls=%fused_computation.22 | convolution fusion | flops 6457131008 | bytes 29556736 | tf_op jit(solution)/shard_map/rcpqk,kn->rcpqn/dot_general | solution.py:21
  183.6 15.3 %copy.46 = bf16[2,8,2,48,1024]{3,2,1,0,4:T(2,128)(2,1)} copy(bf16[2,8,2,48,1024]{4,3,2,1,0:T(8,128)(2,1)S(1)} %pad_maximum_fusion.3) | data formatting | bytes 6291456 | tf_op jit(solution)/shard_map/stack | solution.py:26
  198.8 16.5 %reshape.62 = bf16[16,2,49152]{2,1,0:T(2,128)(2,1)} reshape(bf16[1024,2,8,2,48]{4,3,2,1,0:T(2,128)(2,1)} %bitcast.85) | data formatting | bytes 6291456
  223.4 66.9 %all-to-all-done.1 = bf16[16,2,49152]{2,1,0:T(2,128)(2,1)S(1)} async-done(((bf16[16,2,49152]{2,1,0:T(2,128)(2,1)}), bf16[16,2,49152]{2,1,0:T(2,128)(2,1)S(1)}, u32[]{:S(2)}, u32[]{:S(2)}) %all-to-all-start.1) | async-done | bytes 3145760 | tf_op jit(solution)/shard_map/all_to_all | solution.py:166
  290.3 11.3 %reshape.63 = bf16[1024,2,8,2,48]{4,3,2,1,0:T(2,128)(2,1)} reshape(bf16[16,2,49152]{2,1,0:T(2,128)(2,1)S(1)} %all-to-all-done.1) | data formatting | bytes 6291456
  301.6 12.0 %copy.78 = bf16[2,8,2,48,16,64]{3,4,5,2,1,0:T(8,128)(2,1)} copy(bf16[2,8,2,48,16,64]{3,2,1,0,5,4:T(2,128)(2,1)} %bitcast.86) | data formatting | bytes 6291456 | tf_op jit(solution)/shard_map/all_to_all | solution.py:166
  313.6 12.8 %all_to_all.33 = bf16[2,8,2,768,64]{3,4,2,1,0:T(8,128)(2,1)} reshape(bf16[2,8,2,16,48,64]{4,3,5,2,1,0:T(8,128)(2,1)} %bitcast.87) | data formatting | bytes 6291456 | tf_op jit(solution)/shard_map/all_to_all | solution.py:166
  355.6 10.5 %copy.49 = bf16[2,64,2,16,384]{1,3,2,4,0:T(8,128)(2,1)} copy(bf16[2,64,2,16,384]{4,3,0,1,2:T(8,128)(2,1)S(1)} %bitcast.95) | data formatting | bytes 6291456 | tf_op jit(solution)/shard_map/transpose | solution.py:113
  384.2 9.6 %copy.50 = bf16[2,4,32,512]{3,2,1,0:T(8,128)(2,1)} copy(bf16[2,4,32,512]{1,2,3,0:T(8,128)(2,1)} %get-tuple-element.10) | data formatting | bytes 524288 | tf_op jit(solution)/shard_map/slice | solution.py:125
  397.0 10.1 %copy.51 = bf16[2,4,32,512]{3,2,1,0:T(8,128)(2,1)} copy(bf16[2,4,32,512]{1,2,3,0:T(8,128)(2,1)} %get-tuple-element.11) | data formatting | bytes 524288 | tf_op jit(solution)/shard_map/slice | solution.py:126
  421.8 14.7 %copy.52 = bf16[2,4,32,512]{1,2,3,0:T(8,128)(2,1)} copy(bf16[2,4,32,512]{3,2,1,0:T(8,128)(2,1)} %collective-permute-done.2) | data formatting | bytes 524288 | tf_op jit(solution)/shard_map/ppermute | solution.py:125
  436.5 14.7 %copy.53 = bf16[2,4,32,512]{1,2,3,0:T(8,128)(2,1)} copy(bf16[2,4,32,512]{3,2,1,0:T(8,128)(2,1)} %collective-permute-done.3) | data formatting | bytes 524288 | tf_op jit(solution)/shard_map/ppermute | solution.py:126
  451.2 15.9 %pad_maximum_fusion.1 = bf16[2,72,32,512]{1,2,3,0:T(8,128)(2,1)} fusion(bf16[2,4,32,512]{1,2,3,0:T(8,128)(2,1)} %copy.53, bf16[2,64,32,4]{1,2,3,0:T(8,128)(2,1)S(1)} %copy-done.8, bf16[2,64,32,120]{1,2,3,0:T(8,128)(2,1)S(1)} %broadcast_in_dim.2, bf16[2,64,32,4]{1,2,3,0:T(8,128)(2,1)S(1)} %copy-done.6, bf16[2,64,32,384]{1,2,3,0:T(8,128)(2,1)} %bitcast.84, ...), kind=kLoop, calls=%fused_computation.1 | loop fusion | flops 28311552 | bytes 9437184 | tf_op jit(solution)/shard_map/concatenate | solution.py:127
  467.1 14.5 %copy.54 = bf16[2,72,32,512]{3,2,1,0:T(8,128)(2,1)} copy(bf16[2,72,32,512]{1,2,3,0:T(8,128)(2,1)} %pad_maximum_fusion.1) | data formatting | bytes 9437184 | tf_op jit(solution)/shard_map/concatenate | solution.py:127
  481.6 57.8 %shard_map.95 = bf16[2,2048,384]{2,1,0:T(8,128)(2,1)} custom-call(s32[2]{0:T(128)} %pad_add_fusion.place_ref, bf16[2,2304,512]{2,1,0:T(8,128)(2,1)} %bitcast.93, bf16[4,3,192,256]{3,2,1,0:T(8,128)(2,1)} %pad_dynamic-update-slice_fusion.weight_ref, bf16[4,192,192]{2,1,0:T(8,128)(2,1)} %broadcast_multiply_fusion.mixer_ref, f32[4,192,1]{2,1,0:T(8,128)} %tile.10.bias_ref), custom_call_target="tpu_custom_call" | custom-call | tf_op jit(solution)/shard_map/pallas_call | solution.py:134
  (93 shorter events, 102.4 us)
Async XLA Ops:
  7.2 341.9 %copy-start = (f32[32,2]{0,1:T(2,128)S(1)}, f32[32,2]{0,1:T(2,128)}, u32[]{:S(2)}) copy-start(f32[32,2]{0,1:T(2,128)} %param.12) | copy-start | bytes 772
  17.2 7.5 %copy-start.1 = (bf16[768,768]{1,0:T(8,128)(2,1)}, bf16[768,768]{1,0:T(8,128)(2,1)S(1)}, u32[]{:S(2)}) copy-start(bf16[768,768]{1,0:T(8,128)(2,1)S(1)} %get-tuple-element.24) | copy-start | bytes 3538948
  17.2 7.5 %copy-start.3 = (bf16[768,768]{1,0:T(8,128)(2,1)}, bf16[768,768]{1,0:T(8,128)(2,1)S(1)}, u32[]{:S(2)}) copy-start(bf16[768,768]{1,0:T(8,128)(2,1)S(1)} %get-tuple-element.25) | copy-start | bytes 3538948
  55.3 7.1 %copy-start.10 = (s32[48,1024]{1,0:T(8,128)S(1)}, s32[48,1024]{1,0:T(8,128)}, u32[]{:S(2)}) copy-start(s32[48,1024]{1,0:T(8,128)} %param.11) | copy-start | bytes 589828
  55.3 78.2 %all-to-all-start = ((bf16[16,2,49152]{2,1,0:T(2,128)(2,1)}), bf16[16,2,49152]{2,1,0:T(2,128)(2,1)S(1)}, u32[]{:S(2)}, u32[]{:S(2)}) async-start(bf16[16,2,49152]{2,1,0:T(2,128)(2,1)} %reshape.60), calls=%async_computation | async-start | bytes 6291456 | tf_op jit(solution)/shard_map/all_to_all | solution.py:159
  215.4 4.7 copy-start.9
  215.4 74.9 %all-to-all-start.1 = ((bf16[16,2,49152]{2,1,0:T(2,128)(2,1)}), bf16[16,2,49152]{2,1,0:T(2,128)(2,1)S(1)}, u32[]{:S(2)}, u32[]{:S(2)}) async-start(bf16[16,2,49152]{2,1,0:T(2,128)(2,1)} %reshape.62), calls=%async_computation.1 | async-start | bytes 6291456 | tf_op jit(solution)/shard_map/all_to_all | solution.py:166
  220.1 126.6 %reduce-scatter.4.cloned.1.call-start = ((), (), s32[]{:S(2)}) async-start(), calls=%async_computation.3 | async-start | bytes 589824
  313.6 12.8 %copy-start.2 = (bf16[768,768]{1,0:T(8,128)(2,1)S(1)}, bf16[768,768]{1,0:T(8,128)(2,1)}, u32[]{:S(2)}) copy-start(bf16[768,768]{1,0:T(8,128)(2,1)} %copy-done.1) | copy-start | bytes 3538948
  313.6 20.3 %slice-start = ((s8[6291456]{0:T(1024)(128)(4,1)}), s8[2097152]{0:T(1024)(128)(4,1)S(1)}, s32[]{:S(2)}) async-start(s8[6291456]{0:T(1024)(128)(4,1)} %bitcast.91), calls=%async_computation.4 | async-start | bytes 4194304
  326.4 7.5 %slice-start.1 = ((s8[6291456]{0:T(1024)(128)(4,1)}), s8[4194304]{0:T(1024)(128)(4,1)S(1)}, s32[]{:S(2)}) async-start(s8[6291456]{0:T(1024)(128)(4,1)} %bitcast.91), calls=%async_computation.5 | async-start | bytes 8388608
  336.3 1.9 copy-start.4
  367.0 3.4 collective-permute-start
  369.0 3.1 collective-permute-start.1
  370.4 6.7 %copy-start.5 = (bf16[2,64,32,4]{1,2,3,0:T(8,128)(2,1)}, bf16[2,64,32,4]{1,2,3,0:T(8,128)(2,1)S(1)}, u32[]{:S(2)}) copy-start(bf16[2,64,32,4]{1,2,3,0:T(8,128)(2,1)S(1)} %collective-permute-done) | copy-start | bytes 98308
  372.2 4.9 copy-start.7
  393.9 28.0 %collective-permute-start.2 = (bf16[2,4,32,512]{3,2,1,0:T(8,128)(2,1)}, bf16[2,4,32,512]{3,2,1,0:T(8,128)(2,1)}, u32[]{:S(2)}, u32[]{:S(2)}) collective-permute-start(bf16[2,4,32,512]{3,2,1,0:T(8,128)(2,1)} %copy.50), channel_id=1, source_target_pairs={{0,2},{2,4},{4,6},{6,8},{8,10},{10,12},{12,14},{14,16},{16,18},{18... | collective-permute-start | bytes 786440 | tf_op jit(solution)/shard_map/ppermute | solution.py:125
  397.0 12.8 %copy-start.11 = (bf16[4,16,16]{2,1,0:T(8,128)(2,1)S(1)}, bf16[4,16,16]{2,1,0:T(8,128)(2,1)}, u32[]{:S(2)}) copy-start(bf16[4,16,16]{2,1,0:T(8,128)(2,1)} %param.15) | copy-start | bytes 6148
  407.1 29.5 %collective-permute-start.3 = (bf16[2,4,32,512]{3,2,1,0:T(8,128)(2,1)}, bf16[2,4,32,512]{3,2,1,0:T(8,128)(2,1)}, u32[]{:S(2)}, u32[]{:S(2)}) collective-permute-start(bf16[2,4,32,512]{3,2,1,0:T(8,128)(2,1)} %copy.51), channel_id=1, source_target_pairs={{2,0},{4,2},{6,4},{8,6},{10,8},{12,10},{14,12},{16,14},{18,16},{20... | collective-permute-start | bytes 786440 | tf_op jit(solution)/shard_map/ppermute | solution.py:126
  412.2 5.6 %copy-start.12 = (f32[4,16]{1,0:T(4,128)S(1)}, f32[4,16]{1,0:T(4,128)}, u32[]{:S(2)}) copy-start(f32[4,16]{1,0:T(4,128)} %param.14) | copy-start | bytes 772
  436.5 14.7 %copy-start.6 = (bf16[2,64,32,4]{1,2,3,0:T(8,128)(2,1)S(1)}, bf16[2,64,32,4]{1,2,3,0:T(8,128)(2,1)}, u32[]{:S(2)}) copy-start(bf16[2,64,32,4]{1,2,3,0:T(8,128)(2,1)} %copy-done.5) | copy-start | bytes 98308
  436.5 14.7 %copy-start.8 = (bf16[2,64,32,4]{1,2,3,0:T(8,128)(2,1)S(1)}, bf16[2,64,32,4]{1,2,3,0:T(8,128)(2,1)}, u32[]{:S(2)}) copy-start(bf16[2,64,32,4]{1,2,3,0:T(8,128)(2,1)} %copy-done.7) | copy-start | bytes 98308
Sparse Core Ops, SparseCore 0:
  338.3 8.3 reduce-scatter.3

commit v2 on v1

--- a/solution.py
+++ b/solution.py
@@ -10,20 +10,185 @@
 
 
 def dft_table(length):
-    index = lax.iota(jnp.int32, length)
-    product = index[:, None] * index[None, :] % length
-    angle = product.astype(jnp.float32) * (2.0 * math.pi / length)
+    inner = 32
+    column = lax.iota(jnp.int32, length)[None, :]
+    fine = lax.iota(jnp.int32, inner)[:, None] * column % length
+    coarse = (lax.iota(jnp.int32, length // inner)[:, None] * inner) * column % length
+    unit = 2.0 * math.pi / length
+    fine = fine.astype(jnp.float32) * unit
+    coarse = coarse.astype(jnp.float32) * unit
     scale = 1.0 / math.sqrt(length)
-    return jnp.concatenate([jnp.cos(angle) * scale, jnp.sin(angle) * scale], axis=1).astype(jnp.bfloat16)
-
-
-def transform(stacked, table, length, sign, form):
-    result = jnp.einsum(form, stacked.astype(jnp.bfloat16), table, preferred_element_type=jnp.float32)
-    real_cos = result[0, ..., :length]
-    real_sin = result[0, ..., length:]
-    imag_cos = result[1, ..., :length]
-    imag_sin = result[1, ..., length:]
-    return jnp.stack([real_cos - sign * imag_sin, imag_cos + sign * real_sin])
+    fine_cos, fine_sin, coarse_cos, coarse_sin = lax.optimization_barrier(
+        (jnp.cos(fine), jnp.sin(fine), jnp.cos(coarse) * scale, jnp.sin(coarse) * scale)
+    )
+    fine_cos, fine_sin = fine_cos[None], fine_sin[None]
+    coarse_cos, coarse_sin = coarse_cos[:, None], coarse_sin[:, None]
+    table = jnp.stack([coarse_cos * fine_cos - coarse_sin * fine_sin, coarse_sin * fine_cos + coarse_cos * fine_sin])
+    return table.astype(jnp.bfloat16).reshape(2, length, length)
+
+
+def gradient_body(spaces, coils, estimate_ref, sens_ref, kdata_ref, mask_ref, par_ref, pe_ref, out_ref,
+                  seen, whole, send_out, got_out, send_back, got_back, total, part, parts,
+                  seen_sent, seen_got, out_sent, out_got, back_sent, back_got, part_sent, part_got):
+    space = lax.axis_index("space")
+    coil = lax.axis_index("coil")
+    f32, bf16 = jnp.float32, jnp.bfloat16
+    width = estimate_ref.shape[2]
+    count, positions, rows, npar = sens_ref.shape[1:]
+    held, npe = kdata_ref.shape[3:]
+    sites = positions * rows
+    lines = positions * held
+
+    barrier = pltpu.get_barrier_semaphore()
+
+    @pl.loop(1, spaces)
+    def _(offset):
+        pl.semaphore_signal(barrier, inc=1, device_id={"space": lax.rem(space + offset, spaces)},
+                            device_id_type=pl.DeviceIdType.MESH)
+
+    for offset in range(1, coils):
+        pl.semaphore_signal(barrier, inc=1, device_id={"coil": lax.rem(coil + offset, coils)},
+                            device_id_type=pl.DeviceIdType.MESH)
+    pl.semaphore_wait(barrier, spaces + coils - 2)
+
+    def to_coil(source, target, offset, sent, got):
+        return pltpu.make_async_remote_copy(
+            src_ref=source, dst_ref=target, send_sem=sent.at[offset], recv_sem=got.at[offset],
+            device_id={"coil": lax.rem(coil + offset, coils)}, device_id_type=pl.DeviceIdType.MESH)
+
+    def to_space(buffer, target, c, offset, sent, got):
+        other = lax.rem(space + offset, spaces)
+        return pltpu.make_async_remote_copy(
+            src_ref=buffer.at[c, other], dst_ref=target.at[c, space], send_sem=sent.at[c], recv_sem=got.at[c],
+            device_id={"space": other}, device_id_type=pl.DeviceIdType.MESH)
+
+    def all_of(buffer, c, sem):
+        span = buffer.at[c, pl.ds(0, spaces - 1)]
+        pltpu.make_async_copy(span, span, sem.at[c]).wait()
+
+    for offset in range(1, coils):
+        to_coil(estimate_ref, seen.at[coil], offset, seen_sent, seen_got).start()
+    seen[coil] = estimate_ref[...]
+    for offset in range(1, coils):
+        to_coil(estimate_ref, seen.at[coil], offset, seen_sent, seen_got).wait()
+    for part_of in range(2):
+        whole[part_of] = jnp.concatenate([seen[j, part_of].astype(f32) for j in range(coils)], axis=-1)
+
+    @pl.loop(0, count)
+    def _(c):
+        profile_real = sens_ref[0, c].reshape(sites, npar)
+        profile_imag = sens_ref[1, c].reshape(sites, npar)
+        real = profile_real * whole[0] - profile_imag * whole[1]
+        imag = profile_real * whole[1] + profile_imag * whole[0]
+        plain = jnp.concatenate([real, imag], axis=0).astype(bf16)
+        turned = jnp.concatenate([imag, -real], axis=0).astype(bf16)
+        along = (((1,), (1,)), ((), ()))
+        spectrum = lax.dot_general(par_ref[0], plain, along, preferred_element_type=f32)
+        spectrum += lax.dot_general(par_ref[1], turned, along, preferred_element_type=f32)
+        send_out[c] = spectrum.reshape(spaces, held, 2 * sites).astype(bf16)
+
+        @pl.loop(1, spaces)
+        def _(offset):
+            to_space(send_out, got_out, c, offset, out_sent, out_got).start()
+
+        got_out[c, space] = send_out[c, space]
+
+    @pl.loop(0, count)
+    def _(c):
+        all_of(got_out, c, out_got)
+        blocks = [got_out[c, s].astype(f32) for s in range(spaces)]
+        grid = [
+            jnp.concatenate([block[:, k * rows:(k + 1) * rows] for block in blocks], axis=-1)
+            for k in range(2 * positions)
+        ]
+        real = jnp.concatenate(grid[:positions], axis=0)
+        imag = jnp.concatenate(grid[positions:], axis=0)
+        plain = jnp.concatenate([real, imag], axis=0).astype(bf16)
+        turned = jnp.concatenate([imag, -real], axis=0).astype(bf16)
+        full = jnp.dot(plain, pe_ref[0], preferred_element_type=f32)
+        full += jnp.dot(turned, pe_ref[1], preferred_element_type=f32)
+        sampled = jnp.concatenate([mask_ref[...].astype(f32)] * positions, axis=0)
+        real = sampled * (full[:lines] - kdata_ref[0, c].reshape(lines, npe))
+        imag = sampled * (full[lines:] - kdata_ref[1, c].reshape(lines, npe))
+        plain = jnp.concatenate([real, imag], axis=0).astype(bf16)
+        turned = jnp.concatenate([-imag, real], axis=0).astype(bf16)
+        back = jnp.dot(plain, pe_ref[0], preferred_element_type=f32)
+        back += jnp.dot(turned, pe_ref[1], preferred_element_type=f32)
+        for s in range(spaces):
+            send_back[c, s] = jnp.concatenate(
+                [back[k * held:(k + 1) * held, s * rows:(s + 1) * rows] for k in range(2 * positions)], axis=-1
+            ).astype(bf16)
+
+        @pl.loop(1, spaces)
+        def _(offset):
+            to_space(send_back, got_back, c, offset, back_sent, back_got).start()
+
+        got_back[c, space] = send_back[c, space]
+
+    total[...] = jnp.zeros_like(total)
+
+    @pl.loop(0, count)
+    def _(c):
+        all_of(got_back, c, back_got)
+        plain = got_back[c].astype(f32).reshape(npar, 2 * sites)
+        turned = jnp.concatenate([-plain[:, sites:], plain[:, :sites]], axis=-1).astype(bf16)
+        along = (((0,), (0,)), ((), ()))
+        image = lax.dot_general(plain.astype(bf16), par_ref[0], along, preferred_element_type=f32)
+        image += lax.dot_general(turned, par_ref[1], along, preferred_element_type=f32)
+        real, imag = image[:sites], image[sites:]
+        profile_real = sens_ref[0, c].reshape(sites, npar)
+        profile_imag = sens_ref[1, c].reshape(sites, npar)
+        total[0] += profile_real * real + profile_imag * imag
+        total[1] += profile_real * imag - profile_imag * real
+
+    for j in range(coils):
+        for part_of in range(2):
+            part[j, part_of] = total[part_of, :, j * width:(j + 1) * width].astype(bf16)
+    for offset in range(1, coils):
+        to_coil(part.at[lax.rem(coil + offset, coils)], parts.at[coil], offset, part_sent, part_got).start()
+    parts[coil] = part[coil]
+    for offset in range(1, coils):
+        to_coil(part.at[lax.rem(coil + offset, coils)], parts.at[coil], offset, part_sent, part_got).wait()
+    result = parts[0].astype(f32)
+    for j in range(1, coils):
+        result += parts[j].astype(f32)
+    out_ref[...] = result
+
+    @pl.loop(0, count)
+    def _(c):
+        all_of(send_out, c, out_sent)
+        all_of(send_back, c, back_sent)
+
+
+def find_gradient(state, sens, kdata, mask):
+    spaces, coils = lax.axis_size("space"), lax.axis_size("coil")
+    _, positions, rows, width = state.shape
+    count, npar = sens.shape[1], sens.shape[4]
+    held, npe = kdata.shape[3:]
+    sites = positions * rows
+    bf16, f32 = jnp.bfloat16, jnp.float32
+    vmem = pl.BlockSpec(memory_space=pltpu.VMEM)
+    dma = pltpu.SemaphoreType.DMA
+    message = pltpu.VMEM((count, spaces, held, 2 * sites), bf16)
+    result = pl.pallas_call(
+        functools.partial(gradient_body, spaces, coils),
+        out_shape=jax.ShapeDtypeStruct((2, sites, width), f32),
+        in_specs=[vmem] * 6,
+        out_specs=vmem,
+        scratch_shapes=[
+            pltpu.VMEM((coils, 2, sites, width), bf16),
+            pltpu.VMEM((2, sites, npar), f32),
+            message, message, message, message,
+            pltpu.VMEM((2, sites, npar), f32),
+            pltpu.VMEM((coils, 2, sites, width), bf16),
+            pltpu.VMEM((coils, 2, sites, width), bf16),
+            dma((coils,)), dma((coils,)), dma((count,)), dma((count,)),
+            dma((count,)), dma((count,)), dma((coils,)), dma((coils,)),
+        ],
+        compiler_params=pltpu.CompilerParams(
+            collective_id=0, has_side_effects=True, vmem_limit_bytes=60 * 1024 * 1024),
+    )(state[0:2].reshape(2, sites, width), sens, kdata, mask, dft_table(npar), dft_table(npe))
+    return result.reshape(2, positions, rows, width)
 
 
 HALO = 4
@@ -149,32 +314,7 @@
 def per_device(state, sens, kdata, mask, inject, kernels, biases, mixers):
     npar = sens.shape[4]
     npe = kdata.shape[4]
-    estimate = lax.all_gather(state[0:2], "coil", axis=3, tiled=True).astype(jnp.float32)
-    coil_real = sens[0] * estimate[0][None] - sens[1] * estimate[1][None]
-    coil_imag = sens[0] * estimate[1][None] + sens[1] * estimate[0][None]
-    coil_images = jnp.stack([coil_real, coil_imag])
-    par_table = dft_table(npar)
-    pe_table = dft_table(npe)
-    columns_done = transform(coil_images, par_table, npar, -1.0, "rcpqn,nk->rcpqk")
-    spectra = lax.all_to_all(
-        columns_done.astype(jnp.bfloat16), "space", split_axis=4, concat_axis=3, tiled=True
-    ).astype(columns_done.dtype)
-    full = transform(spectra, pe_table, npe, -1.0, "rcpnq,nk->rcpqk")
-    sampled = mask.astype(jnp.float32)
-    residual = sampled * (full - kdata)
-    lines = transform(residual, pe_table, npe, 1.0, "rcpqk,kn->rcpqn")
-    returned = lax.all_to_all(
-        lines.astype(jnp.bfloat16), "space", split_axis=4, concat_axis=3, tiled=True
-    ).astype(lines.dtype)
-    images = transform(returned, par_table, npar, 1.0, "rcpkn,kq->rcpnq")
-    part_real = jnp.sum(sens[0] * images[0] + sens[1] * images[1], axis=0)
-    part_imag = jnp.sum(sens[0] * images[1] - sens[1] * images[0], axis=0)
-    gradient = lax.psum_scatter(
-        jnp.stack([part_real, part_imag]).astype(jnp.bfloat16),
-        "coil",
-        scatter_dimension=3,
-        tiled=True,
-    ).astype(jnp.float32)
+    gradient = find_gradient(state, sens, kdata, mask)
     added = jnp.einsum("cg,gpqr->cpqr", inject, gradient, precision=lax.Precision.HIGHEST)
     merged = (state.astype(jnp.float32) + added).astype(jnp.bfloat16)
     new_state = couple(merged, kernels, biases, mixers, npe, npar)

time: 562 us -> 365 us (0.65); the launches traced: 551 us -> 364 us
  Pallas kernels: 57.8 us -> 212 us
  local copies, waits for them, and re-layouts: 228 us -> 100 us
  waiting for transfers between devices: 125 us -> 0.01 us
  other arithmetic: 63.1 us -> 30.6 us
  matrix products: 39.3 us -> 9.24 us
  between operations: 14.6 us -> 0.91 us
  starting transfers between devices: 20.4 us -> 11.5 us
    pallas_call x0 -> x1, Pallas kernels: none -> 154 us  [find_gradient(): pl.pallas_call(functools.partial(gradient_body, spaces, coils), out_shape...]
    all_to_all x2 -> x0, waiting for transfers between devices: 120 us -> none  [the longest x1 66.9 us: per_device(): lax.all_to_all(lines.astype(jnp.bfloat16), 'space', split_axis=4, concat_...]
    unnamed x45 -> x20, local copies, waits for them, and re-layouts: 58.1 us -> 3.73 us
    all_to_all x4 -> x0, local copies, waits for them, and re-layouts: 42.4 us -> none  [the longest x2 24.8 us: per_device(): lax.all_to_all(lines.astype(jnp.bfloat16), 'space', split_axis=4, concat_...]
    dot_general x4 -> x0, matrix products: 32.7 us -> none  [transform(): jnp.einsum(form, stacked.astype(jnp.bfloat16), table, preferred_element_t...]
    another operation x8 -> x4, other arithmetic: 34.6 us -> 6.07 us  [the longest x2 3.93 us: dft_table(): jnp.stack([coarse_cos * fine_cos - coarse_sin * fine_sin, coarse_sin * fi...]
    another operation x2 -> x0, local copies, waits for them, and re-layouts: 26.7 us -> none  [transform(): return jnp.stack([real_cos - sign * imag_sin, imag_cos + sign * real_sin])]
    all_to_all x2 -> x0, starting transfers between devices: 11.7 us -> none  [the longest x1 7.05 us: per_device(): lax.all_to_all(columns_done.astype(jnp.bfloat16), 'space', split_axis=4,...]
  transfers between devices with their start and end apart: 7 -> 4, of which waited for: 4 -> 0; matrix products, arithmetic and copies ran while one was open for 12% -> 10% of each run, Pallas kernels for 0% -> 0%
where the time goes in v2:
time: 365 us; the launch traced here: 364 us
  Pallas kernels  212 us (58%)
  local copies, waits for them, and re-layouts  100 us (27%)
  other arithmetic  30.6 us (8%)
  starting transfers between devices  11.5 us (3%)
  matrix products  9.24 us (3%)
    pallas_call x1, Pallas kernels, find_gradient(): pl.pallas_call(functools.partial(gradient_body, spaces, coils), out_shape...  154 us
    pallas_call x1, Pallas kernels, couple(): pl.pallas_call(functools.partial(couplings_body, layers, rows, width, lan...  57.8 us
    slice x2, local copies, waits for them, and re-layouts, couple(): above = lax.ppermute(cells[:, rows - HALO:], 'space', up)  16.8 us
    concatenate x1, other arithmetic, couple(): cells = jnp.concatenate([above, cells, below], axis=1)  15.9 us
    ppermute x1, local copies, waits for them, and re-layouts, couple(): below = lax.ppermute(cells[:, :HALO], 'space', down)  14.7 us
    ppermute x1, local copies, waits for them, and re-layouts, couple(): above = lax.ppermute(cells[:, rows - HALO:], 'space', up)  14.6 us
    concatenate x1, local copies, waits for them, and re-layouts, couple(): cells = jnp.concatenate([above, cells, below], axis=1)  14.5 us
    transpose x1, local copies, waits for them, and re-layouts, couple(): jnp.transpose(merged.reshape(2, half, positions, rows, width), (0, 3, 2,...  10.5 us
  transfers between devices with their start and end apart: 4, of which 0 were waited for; matrix products, arithmetic and copies ran while one was open for 10% of the time, Pallas kernels for 0%

profile of v2, /device:TPU:15, one launch (start us, length us, event | category | flops | bytes accessed | tf_op | source)
XLA Modules:
  0.0 364.1 jit_solution(15035452284275473604)
XLA Ops:
  1.6 1.6 slice.34
  5.4 1.6 pad_maximum_fusion.3.par_ref
  7.0 1.4 subtract_convert_fusion
  8.4 2.3 pad_maximum_fusion.2.pe_ref
  10.7 153.7 %shard_map.95 = f32[2,128,384]{2,1,0:T(8,128)} custom-call(bf16[2,128,384]{2,1,0:T(8,128)(2,1)} %bitcast.54, f32[2,8,2,64,768]{4,3,2,1,0:T(8,128)} %sens_ref.1, f32[2,8,2,48,1024]{4,3,2,1,0:T(8,128)} %kdata_ref.1, s32[48,1024]{1,0:T(8,128)} %mask_ref.1, bf16[2,768,768]{2,1,0:T(8,128)(2,1)} %pad_maximum_fusion.3.par_ref, ...), custom_call_target="tpu_custom_call" | custom-call | tf_op jit(solution)/shard_map/pallas_call | solution.py:173
  164.4 9.2 %fusion = bf16[32,2,64,384]{3,0,2,1:T(8,128)(2,1)S(1)} fusion(bf16[32,2,64,384]{3,2,1,0:T(8,128)(2,1)} %param.8, f32[2,2,64,384]{3,2,1,0:T(8,128)} %bitcast.50, f32[32,2]{0,1:T(2,128)S(1)} %copy-done), kind=kOutput, calls=%fused_computation.3 | convolution fusion | flops 42467328 | bytes 6684928 | tf_op jit(solution)/shard_map/cg,gpqr->cpqr/dot_general | solution.py:318
  173.7 10.5 %copy.35 = bf16[2,64,2,16,384]{1,3,2,4,0:T(8,128)(2,1)} copy(bf16[2,64,2,16,384]{4,3,0,1,2:T(8,128)(2,1)S(1)} %bitcast.45) | data formatting | bytes 6291456 | tf_op jit(solution)/shard_map/transpose | solution.py:278
  185.0 1.3 collective-permute-start.1
  186.3 3.0 collective-permute-start
  189.3 1.5 copy.41
  193.1 4.6 %pad_maximum_fusion = bf16[2,64,32,512]{1,2,3,0:T(8,128)(2,1)S(1)} fusion(bf16[2,64,32,4]{1,2,3,0:T(8,128)(2,1)S(1)} %collective-permute-done.1, bf16[2,64,32,120]{1,2,3,0:T(8,128)(2,1)S(1)} %broadcast_in_dim.2, bf16[2,64,32,4]{1,2,3,0:T(8,128)(2,1)S(1)} %collective-permute-done, bf16[2,64,32,384]{1,2,3,0:T(8,128)(2,1)} %bitcast.41), kind=kLoop, calls=%fused_computation | loop fusion | flops 6291456 | bytes 8388608 | tf_op jit(solution)/shard_map/concatenate | solution.py:286
  197.7 7.2 %fusion.30 = (bf16[2,4,32,512]{1,2,3,0:T(8,128)(2,1)}, bf16[2,4,32,512]{1,2,3,0:T(8,128)(2,1)}) fusion(bf16[2,64,32,512]{1,2,3,0:T(8,128)(2,1)S(1)} %pad_maximum_fusion), kind=kLoop, calls=%fused_computation.72 | loop fusion | bytes 1048576 | tf_op jit(solution)/shard_map/slice | solution.py:290
  204.9 9.7 %copy.37 = bf16[2,4,32,512]{3,2,1,0:T(8,128)(2,1)} copy(bf16[2,4,32,512]{1,2,3,0:T(8,128)(2,1)} %get-tuple-element.19) | data formatting | bytes 524288 | tf_op jit(solution)/shard_map/slice | solution.py:291
  214.5 2.2 collective-permute-start.3
  216.7 9.7 %copy.36 = bf16[2,4,32,512]{3,2,1,0:T(8,128)(2,1)} copy(bf16[2,4,32,512]{1,2,3,0:T(8,128)(2,1)} %get-tuple-element.18) | data formatting | bytes 524288 | tf_op jit(solution)/shard_map/slice | solution.py:290
  226.4 5.0 %collective-permute-start.2 = (bf16[2,4,32,512]{3,2,1,0:T(8,128)(2,1)}, bf16[2,4,32,512]{3,2,1,0:T(8,128)(2,1)}, u32[]{:S(2)}, u32[]{:S(2)}) collective-permute-start(bf16[2,4,32,512]{3,2,1,0:T(8,128)(2,1)} %copy.36), channel_id=1, source_target_pairs={{0,2},{2,4},{4,6},{6,8},{8,10},{10,12},{12,14},{14,16},{16,18},{18... | collective-permute-start | bytes 786440 | tf_op jit(solution)/shard_map/ppermute | solution.py:290
  232.0 2.3 mul.366
  234.4 4.1 %mul.367 = bf16[4,192,192]{2,1,0:T(8,128)(2,1)S(1)} reshape(bf16[4,12,16,12,16]{4,3,2,1,0:T(8,128)(2,1)} %mul.366) | data formatting | bytes 589824 | tf_op jit(solution)/shard_map/mul | solution.py:217
  241.1 14.7 %copy.39 = bf16[2,4,32,512]{1,2,3,0:T(8,128)(2,1)} copy(bf16[2,4,32,512]{3,2,1,0:T(8,128)(2,1)} %collective-permute-done.3) | data formatting | bytes 524288 | tf_op jit(solution)/shard_map/ppermute | solution.py:291
  255.8 14.6 %copy.38 = bf16[2,4,32,512]{1,2,3,0:T(8,128)(2,1)} copy(bf16[2,4,32,512]{3,2,1,0:T(8,128)(2,1)} %collective-permute-done.2) | data formatting | bytes 524288 | tf_op jit(solution)/shard_map/ppermute | solution.py:290
  270.4 15.9 %pad_maximum_fusion.1 = bf16[2,72,32,512]{1,2,3,0:T(8,128)(2,1)} fusion(bf16[2,4,32,512]{1,2,3,0:T(8,128)(2,1)} %copy.39, bf16[2,64,32,4]{1,2,3,0:T(8,128)(2,1)S(1)} %collective-permute-done.1, bf16[2,64,32,120]{1,2,3,0:T(8,128)(2,1)S(1)} %broadcast_in_dim.2, bf16[2,64,32,4]{1,2,3,0:T(8,128)(2,1)S(1)} %collective-permute-done, ...), kind=kLoop, calls=%fused_computation.1 | loop fusion | flops 28311552 | bytes 9437184 | tf_op jit(solution)/shard_map/concatenate | solution.py:292
  286.3 14.5 %copy.40 = bf16[2,72,32,512]{3,2,1,0:T(8,128)(2,1)} copy(bf16[2,72,32,512]{1,2,3,0:T(8,128)(2,1)} %pad_maximum_fusion.1) | data formatting | bytes 9437184 | tf_op jit(solution)/shard_map/concatenate | solution.py:292
  300.8 57.8 %shard_map.96 = bf16[2,2048,384]{2,1,0:T(8,128)(2,1)} custom-call(s32[2]{0:T(128)} %pad_add_fusion.place_ref, bf16[2,2304,512]{2,1,0:T(8,128)(2,1)} %bitcast.43, bf16[4,3,192,256]{3,2,1,0:T(8,128)(2,1)} %copy-done.3, bf16[4,192,192]{2,1,0:T(8,128)(2,1)} %broadcast_multiply_fusion.mixer_ref, f32[4,192,1]{2,1,0:T(8,128)} %tile.10.bias_ref), custom_call_target="tpu_custom_call" | custom-call | tf_op jit(solution)/shard_map/pallas_call | solution.py:299
  358.6 4.7 %copy.46 = bf16[2,16,2,64,384]{4,3,2,1,0:T(8,128)(2,1)} copy(bf16[2,16,2,64,384]{4,1,2,3,0:T(8,128)(2,1)} %bitcast.44) | data formatting | bytes 6291456 | tf_op jit(solution)/shard_map/transpose | solution.py:311
  (45 shorter events, 10.2 us)
Async XLA Ops:
  0.6 163.8 %copy-start = (f32[32,2]{0,1:T(2,128)S(1)}, f32[32,2]{0,1:T(2,128)}, u32[]{:S(2)}) copy-start(f32[32,2]{0,1:T(2,128)} %param.12) | copy-start | bytes 772
  185.0 7.9 %collective-permute-start.1 = (bf16[2,64,32,4]{1,2,3,0:T(8,128)(2,1)S(1)}, bf16[2,64,32,4]{1,2,3,0:T(8,128)(2,1)S(1)}, u32[]{:S(2)}, u32[]{:S(2)}) collective-permute-start(bf16[2,64,32,4]{1,2,3,0:T(8,128)(2,1)S(1)} %get-tuple-element.21), channel_id=1, source_target_pairs={{0,1},{2,3},{4,5},{6,7},{8,9},{10,11},{12,13},{14,15},{16,17},{18,... | collective-permute-start | bytes 98312 | tf_op jit(solution)/shard_map/ppermute | solution.py:283
  186.3 6.6 %collective-permute-start = (bf16[2,64,32,4]{1,2,3,0:T(8,128)(2,1)S(1)}, bf16[2,64,32,4]{1,2,3,0:T(8,128)(2,1)S(1)}, u32[]{:S(2)}, u32[]{:S(2)}) collective-permute-start(bf16[2,64,32,4]{1,2,3,0:T(8,128)(2,1)S(1)} %get-tuple-element.20), channel_id=1, source_target_pairs={{1,0},{3,2},{5,4},{7,6},{9,8},{11,10},{13,12},{15,14},{17,16},{19,... | collective-permute-start | bytes 98312 | tf_op jit(solution)/shard_map/ppermute | solution.py:284
  191.8 1.1 copy-start.3
  214.5 26.6 %collective-permute-start.3 = (bf16[2,4,32,512]{3,2,1,0:T(8,128)(2,1)}, bf16[2,4,32,512]{3,2,1,0:T(8,128)(2,1)}, u32[]{:S(2)}, u32[]{:S(2)}) collective-permute-start(bf16[2,4,32,512]{3,2,1,0:T(8,128)(2,1)} %copy.37), channel_id=1, source_target_pairs={{2,0},{4,2},{6,4},{8,6},{10,8},{12,10},{14,12},{16,14},{18,16},{20... | collective-permute-start | bytes 786440 | tf_op jit(solution)/shard_map/ppermute | solution.py:291
  216.7 15.3 %copy-start.4 = (bf16[4,16,16]{2,1,0:T(8,128)(2,1)S(1)}, bf16[4,16,16]{2,1,0:T(8,128)(2,1)}, u32[]{:S(2)}) copy-start(bf16[4,16,16]{2,1,0:T(8,128)(2,1)} %param.15) | copy-start | bytes 6148
  226.4 12.9 %copy-start.5 = (f32[4,16]{1,0:T(4,128)S(1)}, f32[4,16]{1,0:T(4,128)}, u32[]{:S(2)}) copy-start(f32[4,16]{1,0:T(4,128)} %param.14) | copy-start | bytes 772
  226.4 29.4 %collective-permute-start.2 = (bf16[2,4,32,512]{3,2,1,0:T(8,128)(2,1)}, bf16[2,4,32,512]{3,2,1,0:T(8,128)(2,1)}, u32[]{:S(2)}, u32[]{:S(2)}) collective-permute-start(bf16[2,4,32,512]{3,2,1,0:T(8,128)(2,1)} %copy.36), channel_id=1, source_target_pairs={{0,2},{2,4},{4,6},{6,8},{8,10},{10,12},{12,14},{14,16},{16,18},{18... | collective-permute-start | bytes 786440 | tf_op jit(solution)/shard_map/ppermute | solution.py:290
  300.8 63.3 %copy-start.1 = (f32[32,2]{0,1:T(2,128)S(1)}, f32[32,2]{0,1:T(2,128)}, u32[]{:S(2)}) copy-start(f32[32,2]{0,1:T(2,128)} %param.12) | copy-start | bytes 772
  358.6 4.8 %copy-start.2 = (f32[2,128,384]{2,1,0:T(8,128)S(1)}, f32[2,128,384]{2,1,0:T(8,128)}, u32[]{:S(2)}) copy-start(f32[2,128,384]{2,1,0:T(8,128)} %shard_map.95) | copy-start | bytes 1179652

commit v3 on v2

--- a/solution.py
+++ b/solution.py
@@ -27,7 +27,7 @@
     return table.astype(jnp.bfloat16).reshape(2, length, length)
 
 
-def gradient_body(spaces, coils, estimate_ref, sens_ref, kdata_ref, mask_ref, par_ref, pe_ref, out_ref,
+def gradient_body(spaces, coils, estimate_ref, sens_ref, kdata_ref, mask_ref, par_ref, pe_ref, state_ref, out_ref, cells_ref,
                   seen, whole, send_out, got_out, send_back, got_back, total, part, parts,
                   seen_sent, seen_got, out_sent, out_got, back_sent, back_got, part_sent, part_got):
     space = lax.axis_index("space")
@@ -92,6 +92,17 @@
             to_space(send_out, got_out, c, offset, out_sent, out_got).start()
 
         got_out[c, space] = send_out[c, space]
+
+    half = state_ref.shape[0] // 2
+    group = 16
+
+    @pl.loop(0, rows // group)
+    def _(g):
+        at = pl.ds(pl.multiple_of(g * group, group), group)
+        for side in range(2):
+            for position in range(positions):
+                cells = state_ref[side * half:(side + 1) * half, position, at, :].astype(f32)
+                cells_ref[side, at, position * half:(position + 1) * half, :] = jnp.swapaxes(cells, 0, 1).astype(bf16)
 
     @pl.loop(0, count)
     def _(c):
@@ -170,11 +181,15 @@
     vmem = pl.BlockSpec(memory_space=pltpu.VMEM)
     dma = pltpu.SemaphoreType.DMA
     message = pltpu.VMEM((count, spaces, held, 2 * sites), bf16)
-    result = pl.pallas_call(
+    channels = state.shape[0]
+    result, cells = pl.pallas_call(
         functools.partial(gradient_body, spaces, coils),
-        out_shape=jax.ShapeDtypeStruct((2, sites, width), f32),
-        in_specs=[vmem] * 6,
-        out_specs=vmem,
+        out_shape=(
+            jax.ShapeDtypeStruct((2, sites, width), f32),
+            jax.ShapeDtypeStruct((2, rows, positions * channels // 2, width), bf16),
+        ),
+        in_specs=[vmem] * 7,
+        out_specs=(vmem, vmem),
         scratch_shapes=[
             pltpu.VMEM((coils, 2, sites, width), bf16),
             pltpu.VMEM((2, sites, npar), f32),
@@ -187,8 +202,8 @@
         ],
         compiler_params=pltpu.CompilerParams(
             collective_id=0, has_side_effects=True, vmem_limit_bytes=60 * 1024 * 1024),
-    )(state[0:2].reshape(2, sites, width), sens, kdata, mask, dft_table(npar), dft_table(npe))
-    return result.reshape(2, positions, rows, width)
+    )(state[0:2].reshape(2, sites, width), sens, kdata, mask, dft_table(npar), dft_table(npe), state)
+    return result.reshape(2, positions, rows, width), cells
 
 
 HALO = 4
@@ -202,122 +217,232 @@
     for out_pos in range(2):
         rows.append(jnp.concatenate([taps[:, in_pos - out_pos + 1] for in_pos in range(2)], axis=-1))
     mixed = jnp.concatenate(rows, axis=-2)
-    strip = jnp.concatenate([mixed[:, b] for b in range(3)], axis=-1)
-    unit = 2 * ins
+    strip = jnp.concatenate([mixed[:, b, c] for b in range(3) for c in range(3)], axis=-1)
+    unit = 6 * ins
     bands = [
-        jnp.pad(strip, ((0, 0), (0, 0), (0, 0), (unit * x, unit * (BLOCK - 1 - x)))) for x in range(BLOCK)
+        jnp.pad(strip, ((0, 0), (0, 0), (unit * x, unit * (BLOCK - 1 - x)))) for x in range(BLOCK)
     ]
     return jnp.concatenate(bands, axis=-2)
 
 
 def mixer_weights(mixers):
-    layers, outs, ins = mixers.shape
+    ins = mixers.shape[2]
     times = 2 * BLOCK
-    eye = jnp.eye(times, dtype=mixers.dtype)
-    spread = mixers[:, None, :, None, :] * eye[None, :, None, :, None]
-    return spread.reshape(layers, times * outs, times * ins)
-
-
-def couplings_body(layers, rows, width, lanes, total_rows, total_cols, unit,
-                   place_ref, cells_ref, weight_ref, mixer_ref, bias_ref, out_ref, halves, shifted):
+    bands = [jnp.pad(mixers, ((0, 0), (0, 0), (ins * x, ins * (times - 1 - x)))) for x in range(times)]
+    return jnp.concatenate(bands, axis=-2)
+
+
+def couplings_body(layers, rows, width, lanes, total_rows, total_cols, unit, spaces, coils,
+                   cells_ref, gradient_ref, inject_ref, weight_ref, mixer_ref, bias_ref, out_ref,
+                   halves, shifted, strips, borders, col_sent, col_got, row_sent, row_got):
+    f32, bf16 = jnp.float32, jnp.bfloat16
+    mesh_id = pl.DeviceIdType.MESH
+    space = lax.axis_index("space")
+    coil = lax.axis_index("coil")
+    positions = gradient_ref.shape[1]
     halo_rows = rows + 2 * HALO
-    row_start = place_ref[0] - HALO
-    col_start = place_ref[1]
+    row_start = space * rows - HALO
+    col_start = coil * width
+
+    barrier = pltpu.get_barrier_semaphore()
+    for step in (1, -1):
+        pl.semaphore_signal(barrier, inc=1, device_id={"coil": lax.rem(coil + step + coils, coils)}, device_id_type=mesh_id)
+        pl.semaphore_signal(barrier, inc=1, device_id={"space": lax.rem(space + step + spaces, spaces)}, device_id_type=mesh_id)
+    pl.semaphore_wait(barrier, 4)
+
+    for half in range(2):
+        spare = (halves.shape[1] - halo_rows * unit, lanes)
+        halves[half, halo_rows * unit:, :] = jnp.zeros(spare, bf16)
+
+        @pl.when(space == 0)
+        def _(half=half):
+            halves[half, 0:HALO * unit, :] = jnp.zeros((HALO * unit, lanes), bf16)
+
+        @pl.when(space == spaces - 1)
+        def _(half=half):
+            halves[half, (HALO + rows) * unit:halo_rows * unit, :] = jnp.zeros((HALO * unit, lanes), bf16)
+
+    @pl.loop(0, rows)
+    def _(row):
+        lines = [
+            jnp.concatenate(
+                [
+                    jnp.broadcast_to(gradient_ref[g, p, pl.ds(row, 1), :], (unit // positions, width))
+                    for p in range(positions)
+                ],
+                axis=0,
+            )
+            for g in range(2)
+        ]
+        from_row = pl.ds(pl.multiple_of(row * unit, unit), unit)
+        into = pl.ds(pl.multiple_of((row + HALO) * unit, unit), unit)
+        for half in range(2):
+            added = inject_ref[half, 0] * lines[0] + inject_ref[half, 1] * lines[1]
+            merged = cells_ref[half, row].astype(f32) + added
+            merged = jnp.concatenate([merged, jnp.zeros((unit, lanes - width), f32)], axis=-1)
+            halves[half, into, :] = merged.astype(bf16)
+            strips[0, half, from_row, :] = pltpu.roll(merged, lanes - width, 1)[:, lanes - 128:].astype(bf16)
+            strips[1, half, from_row, :] = pltpu.roll(merged, width, 1)[:, lanes - 128:].astype(bf16)
+
+    def sideways(way):
+        other = lax.rem(coil + (1, coils - 1)[way], coils)
+        return pltpu.make_async_remote_copy(
+            src_ref=strips.at[way], dst_ref=borders.at[way], send_sem=col_sent.at[way], recv_sem=col_got.at[way],
+            device_id={"coil": other}, device_id_type=mesh_id)
+
+    def upright(way, half):
+        other = lax.rem(space + (1, spaces - 1)[way], spaces)
+        source = (rows, HALO)[way] * unit
+        target = (0, HALO + rows)[way] * unit
+        return pltpu.make_async_remote_copy(
+            src_ref=halves.at[half, pl.ds(source, HALO * unit)],
+            dst_ref=halves.at[half, pl.ds(target, HALO * unit)],
+            send_sem=row_sent.at[way, half], recv_sem=row_got.at[way, half],
+            device_id={"space": other}, device_id_type=mesh_id)
+
+    has_left, has_right = coil > 0, coil < coils - 1
+    has_above, has_below = space > 0, space < spaces - 1
+
+    @pl.when(has_right)
+    def _():
+        sideways(0).start()
+
+    @pl.when(has_left)
+    def _():
+        sideways(1).start()
+
+    edge = lax.broadcasted_iota(jnp.int32, (1, 128), 1)
+
+    @pl.when(has_left)
+    def _():
+        sideways(0).wait_recv()
+
+        @pl.loop(0, rows)
+        def _(row):
+            into = pl.ds(pl.multiple_of((row + HALO) * unit, unit), unit)
+            from_row = pl.ds(pl.multiple_of(row * unit, unit), unit)
+            for half in range(2):
+                own = halves[half, into, lanes - 128:].astype(f32)
+                new = borders[0, half, from_row, :].astype(f32)
+                halves[half, into, lanes - 128:] = jnp.where(edge >= 128 - HALO, new, own).astype(bf16)
+
+    @pl.when(has_right)
+    def _():
+        sideways(1).wait_recv()
+        first = width % 128
+
+        @pl.loop(0, rows)
+        def _(row):
+            into = pl.ds(pl.multiple_of((row + HALO) * unit, unit), unit)
+            from_row = pl.ds(pl.multiple_of(row * unit, unit), unit)
+            for half in range(2):
+                own = halves[half, into, lanes - 128:].astype(f32)
+                new = borders[1, half, from_row, :].astype(f32)
+                inside = (edge >= first) & (edge < first + HALO)
+                halves[half, into, lanes - 128:] = jnp.where(inside, new, own).astype(bf16)
+
+    for half in range(2):
+        @pl.when(has_below)
+        def _(half=half):
+            upright(0, half).start()
+
+        @pl.when(has_above)
+        def _(half=half):
+            upright(1, half).start()
+
+    for half in range(2):
+        @pl.when(has_below)
+        def _(half=half):
+            upright(0, half).wait_send()
+            upright(1, half).wait_recv()
+
+        @pl.when(has_above)
+        def _(half=half):
+            upright(1, half).wait_send()
+            upright(0, half).wait_recv()
+
+    @pl.when(has_right)
+    def _():
+        sideways(0).wait_send()
+
+    @pl.when(has_left)
+    def _():
+        sideways(1).wait_send()
+
     lane = lax.broadcasted_iota(jnp.int32, (1, lanes), 1)
     column = jnp.where(lane >= lanes - HALO, lane - lanes, lane) + col_start
     column_ok = jnp.where((column >= 0) & (column < total_cols), 1.0, 0.0)
-    for half in range(2):
-        halves[half, 0:halo_rows * unit, :] = cells_ref[half]
-        halves[half, halo_rows * unit:, :] = jnp.zeros(
-            (halves.shape[1] - halo_rows * unit, lanes), halves.dtype)
-        for side in range(2):
-            shifted[2 * side, halo_rows * unit:, :] = jnp.zeros(
-                (halves.shape[1] - halo_rows * unit, lanes), halves.dtype)
     for layer in range(layers):
         source, target = layer % 2, 1 - layer % 2
 
-        def spread(index, _, source=source):
-            at = pl.ds(pl.multiple_of(index * unit, unit), unit)
-            line = halves[source, at, :].astype(jnp.float32)
-            shifted[0, at, :] = pltpu.roll(line, 1, 1).astype(jnp.bfloat16)
-            shifted[1, at, :] = halves[source, at, :]
-            shifted[2, at, :] = pltpu.roll(line, lanes - 1, 1).astype(jnp.bfloat16)
-            return 0
-
-        lax.fori_loop(0, halves.shape[1] // unit, spread, 0)
+        @pl.loop(0, halves.shape[1] // (2 * unit))
+        def _(pair, source=source):
+            for one in range(2):
+                index = 2 * pair + one
+                at = pl.ds(pl.multiple_of(index * unit, unit), unit)
+                line = halves[source, at, :]
+                wide = line.astype(f32)
+                moved = (pltpu.roll(wide, 1, 1).astype(bf16), line, pltpu.roll(wide, lanes - 1, 1).astype(bf16))
+                for c in range(3):
+                    shifted[pl.ds(pl.multiple_of((3 * index + c) * unit, unit), unit), :] = moved[c]
+
         left = halo_rows - 2 * layer - 2
         steps = -(-left // BLOCK)
 
-        def block(index, _, layer=layer, target=target):
+        @pl.loop(0, steps)
+        def _(index, layer=layer, target=target):
             start = layer + index * BLOCK
-            inside = pl.ds(pl.multiple_of(start * unit, unit), (BLOCK + 2) * unit)
-            raw = jnp.dot(weight_ref[layer, 0], shifted[0, inside, :], preferred_element_type=jnp.float32)
-            raw += jnp.dot(weight_ref[layer, 1], shifted[1, inside, :], preferred_element_type=jnp.float32)
-            raw += jnp.dot(weight_ref[layer, 2], shifted[2, inside, :], preferred_element_type=jnp.float32)
+            inside = pl.ds(pl.multiple_of(start * 3 * unit, 3 * unit), (BLOCK + 2) * 3 * unit)
+            raw = jnp.dot(weight_ref[layer], shifted[inside, :], preferred_element_type=f32)
             hidden = jnp.maximum(raw + bias_ref[layer], 0.0)
             step = lax.broadcasted_iota(jnp.int32, (BLOCK * unit, 1), 0) // unit
             row = step + (start + 1 + row_start)
             row_ok = jnp.where((row >= 0) & (row < total_rows), 1.0, 0.0)
-            hidden = (hidden * row_ok * column_ok).astype(jnp.bfloat16)
-            update = jnp.dot(mixer_ref[layer], hidden, preferred_element_type=jnp.float32)
+            hidden = (hidden * (row_ok * column_ok)).astype(bf16)
+            update = jnp.dot(mixer_ref[layer], hidden, preferred_element_type=f32)
             at = pl.ds(pl.multiple_of((start + 1) * unit, unit), BLOCK * unit)
-            halves[target, at, :] = (halves[target, at, :].astype(jnp.float32) + update).astype(jnp.bfloat16)
-            return 0
-
-        lax.fori_loop(0, steps, block, 0)
+            halves[target, at, :] = (halves[target, at, :].astype(f32) + update).astype(bf16)
+
     for half in range(2):
         out_ref[half] = halves[half, HALO * unit:(HALO + rows) * unit, 0:width]
 
 
-def couple(merged, kernels, biases, mixers, total_rows, total_cols):
-    channels, positions, rows, width = merged.shape
-    half = channels // 2
+def couple(cells, gradient, inject, kernels, biases, mixers, total_rows, total_cols):
+    _, rows, unit, width = cells.shape
+    positions = gradient.shape[1]
+    half = unit // positions
     layers = kernels.shape[0]
-    unit = half * positions
     lanes = -(-(width + 2 * HALO) // 128) * 128
-    cells = jnp.transpose(merged.reshape(2, half, positions, rows, width), (0, 3, 2, 1, 4))
-    cells = cells.reshape(2, rows, unit, width)
-    count = lax.axis_size("coil")
-    up = [(i, i + 1) for i in range(count - 1)]
-    down = [(i + 1, i) for i in range(count - 1)]
-    before = lax.ppermute(cells[..., width - HALO:], "coil", up)
-    after = lax.ppermute(cells[..., :HALO], "coil", down)
-    gap = jnp.zeros(cells.shape[:-1] + (lanes - width - 2 * HALO,), cells.dtype)
-    cells = jnp.concatenate([cells, after, gap, before], axis=-1)
-    count = lax.axis_size("space")
-    up = [(i, i + 1) for i in range(count - 1)]
-    down = [(i + 1, i) for i in range(count - 1)]
-    above = lax.ppermute(cells[:, rows - HALO:], "space", up)
-    below = lax.ppermute(cells[:, :HALO], "space", down)
-    cells = jnp.concatenate([above, cells, below], axis=1)
-    halo_rows = rows + 2 * HALO
-    held = halo_rows + 8
-    cells = cells.reshape(2, halo_rows * unit, lanes)
-    place = jnp.stack([lax.axis_index("space") * rows, lax.axis_index("coil") * width]).astype(jnp.int32)
+    spaces, coils = lax.axis_size("space"), lax.axis_size("coil")
+    held = rows + 2 * HALO + 8
     bias = jnp.tile(biases, (1, positions * BLOCK))[:, :, None]
+    spread = jnp.tile(jnp.transpose(inject.reshape(2, half, 2), (0, 2, 1)), (1, 1, positions))[..., None]
     vmem = pl.BlockSpec(memory_space=pltpu.VMEM)
+    dma = pltpu.SemaphoreType.DMA
     out = pl.pallas_call(
-        functools.partial(couplings_body, layers, rows, width, lanes, total_rows, total_cols, unit),
+        functools.partial(couplings_body, layers, rows, width, lanes, total_rows, total_cols, unit, spaces, coils),
         out_shape=jax.ShapeDtypeStruct((2, rows * unit, width), jnp.bfloat16),
-        in_specs=[pl.BlockSpec(memory_space=pltpu.SMEM)] + [vmem] * 4,
+        in_specs=[vmem] * 6,
         out_specs=vmem,
         scratch_shapes=[
             pltpu.VMEM((2, held * unit, lanes), jnp.bfloat16),
-            pltpu.VMEM((3, held * unit, lanes), jnp.bfloat16),
+            pltpu.VMEM((3 * held * unit, lanes), jnp.bfloat16),
+            pltpu.VMEM((2, 2, rows * unit, 128), jnp.bfloat16),
+            pltpu.VMEM((2, 2, rows * unit, 128), jnp.bfloat16),
+            dma((2,)), dma((2,)), dma((2, 2)), dma((2, 2)),
         ],
-        compiler_params=pltpu.CompilerParams(vmem_limit_bytes=56 * 1024 * 1024),
-    )(place, cells, coupling_weights(kernels), mixer_weights(mixers), bias)
+        compiler_params=pltpu.CompilerParams(
+            collective_id=1, has_side_effects=True, vmem_limit_bytes=56 * 1024 * 1024),
+    )(cells, gradient, spread, coupling_weights(kernels), mixer_weights(mixers), bias)
     out = out.reshape(2, rows, positions, half, width)
-    return jnp.transpose(out, (0, 3, 2, 1, 4)).reshape(channels, positions, rows, width)
+    return jnp.transpose(out, (0, 3, 2, 1, 4)).reshape(2 * half, positions, rows, width)
 
 
 def per_device(state, sens, kdata, mask, inject, kernels, biases, mixers):
     npar = sens.shape[4]
     npe = kdata.shape[4]
-    gradient = find_gradient(state, sens, kdata, mask)
-    added = jnp.einsum("cg,gpqr->cpqr", inject, gradient, precision=lax.Precision.HIGHEST)
-    merged = (state.astype(jnp.float32) + added).astype(jnp.bfloat16)
-    new_state = couple(merged, kernels, biases, mixers, npe, npar)
+    gradient, cells = find_gradient(state, sens, kdata, mask)
+    new_state = couple(cells, gradient, inject, kernels, biases, mixers, npe, npar)
     return (new_state, gradient)
 
 

time: 365 us -> 246 us (0.67)
  local copies, waits for them, and re-layouts: 100 us -> 11.3 us
  other arithmetic: 30.6 us -> 8.56 us
  starting transfers between devices: 11.5 us -> 0 us
  Pallas kernels: 212 us -> 222 us
  matrix products: 9.24 us -> 0 us
    ppermute x2 -> x0, local copies, waits for them, and re-layouts: 29.3 us -> none  [the longest x1 14.7 us: couple(): below = lax.ppermute(cells[:, :HALO], 'space', down)]
    slice x5 -> x0, local copies, waits for them, and re-layouts: 27.4 us -> none  [the longest x2 16.8 us: couple(): above = lax.ppermute(cells[:, rows - HALO:], 'space', up)]
    concatenate x3 -> x0, other arithmetic: 20.6 us -> none  [the longest x1 15.9 us: couple(): cells = jnp.concatenate([above, cells, below], axis=1)]
    concatenate x1 -> x2, local copies, waits for them, and re-layouts: 14.5 us -> 0.23 us  [the longest x1 0.15 us: coupling_weights(): jnp.concatenate([mixed[:, b, c] for b in range(3) for c in range(3)], axi...]
    ppermute x4 -> x0, starting transfers between devices: 11.5 us -> none  [the longest x1 5.01 us: couple(): above = lax.ppermute(cells[:, rows - HALO:], 'space', up)]
    transpose x1, local copies, waits for them, and re-layouts: 10.5 us -> 0.01 us  [couple(): jnp.transpose(inject.reshape(2, half, 2), (0, 2, 1))]
    dot_general x1 -> x0, matrix products: 9.24 us -> none  [per_device(): jnp.einsum('cg,gpqr->cpqr', inject, gradient, precision=lax.Precision.HIG...]
    pallas_call x1, Pallas kernels: 57.8 us -> 66.3 us  [couple(): pl.pallas_call(functools.partial(couplings_body, layers, rows, width, lan...]
  transfers between devices with their start and end apart: 4 -> 0, of which waited for: 0 -> 0; matrix products, arithmetic and copies ran while one was open for 10% -> 0% of each run, Pallas kernels for 0% -> 0%
where the time goes in v3:
time: 246 us; the launch traced here: 243 us
  Pallas kernels  222 us (90%)
  local copies, waits for them, and re-layouts  11.3 us (5%)
  other arithmetic  8.56 us (3%)
    pallas_call x1, Pallas kernels, find_gradient(): pl.pallas_call(functools.partial(gradient_body, spaces, coils), out_shape...  156 us
    pallas_call x1, Pallas kernels, couple(): pl.pallas_call(functools.partial(couplings_body, layers, rows, width, lan...  66.3 us

profile of v3, /device:TPU:15, one launch (start us, length us, event | category | flops | bytes accessed | tf_op | source)
XLA Modules:
  0.0 242.6 jit_solution(15724589970372460515)
XLA Ops:
  0.6 1.6 slice.40
  2.3 0.4 fusion.16
  2.7 0.4 sine_multiply_fusion.1
  3.1 0.8 subtract_convert_fusion.1
  3.8 1.6 pad_maximum_fusion.1.par_ref
  5.4 0.5 fusion.25
  5.9 1.0 sine_multiply_fusion
  7.0 1.4 subtract_convert_fusion
  8.4 2.3 pad_maximum_fusion.pe_ref
  10.7 155.6 %shard_map.95 = (f32[2,128,384]{2,1,0:T(8,128)}, bf16[2,64,32,384]{3,2,1,0:T(8,128)(2,1)}) custom-call(bf16[2,128,384]{2,1,0:T(8,128)(2,1)} %bitcast.47, f32[2,8,2,64,768]{4,3,2,1,0:T(8,128)} %sens_ref.1, f32[2,8,2,48,1024]{4,3,2,1,0:T(8,128)} %kdata_ref.1, s32[48,1024]{1,0:T(8,128)} %mask_ref.1, bf16[2,768,768]{2,1,0:T(8,128)(2,1)} %pad_maximum_fusion.1.par_ref, ...), custom_call_target="tpu_custom_call" | custom-call | tf_op jit(solution)/shard_map/pallas_call | solution.py:185
  166.4 0.7 tile.20.inject_ref
  167.1 0.9 copy.15
  168.1 0.2 maximum_maximum_fusion
  168.3 0.1 concatenate.25
  168.5 0.1 pad_dynamic-update-slice_fusion.4
  168.6 0.1 pad_dynamic-update-slice_fusion.3
  168.7 0.1 pad_dynamic-update-slice_fusion.2
  168.8 0.1 pad_dynamic-update-slice_fusion.weight_ref
  169.2 0.1 constant_dynamic-update-slice_fusion.7
  169.3 0.1 constant_dynamic-update-slice_fusion.6
  169.8 1.0 tile.21.bias_ref
  170.8 66.3 %shard_map.96 = bf16[2,2048,384]{2,1,0:T(8,128)(2,1)} custom-call(bf16[2,64,32,384]{3,2,1,0:T(8,128)(2,1)} %get-tuple-element.20.cells_ref, f32[2,2,64,384]{3,2,1,0:T(8,128)} %bitcast.45, f32[2,2,32,1]{3,2,1,0:T(8,128)} %tile.20.inject_ref, bf16[4,192,768]{2,1,0:T(8,128)(2,1)} %copy-done.1, bf16[4,192,192]{2,1,0:T(8,128)(2,1)} %copy-done.3, ...), custom_call_target="tpu_custom_call" | custom-call | tf_op jit(solution)/shard_map/pallas_call | solution.py:422
  237.1 4.7 %copy.18 = bf16[2,16,2,64,384]{4,3,2,1,0:T(8,128)(2,1)} copy(bf16[2,16,2,64,384]{4,1,2,3,0:T(8,128)(2,1)} %bitcast.38) | data formatting | bytes 6291456 | tf_op jit(solution)/shard_map/transpose | solution.py:438
  241.8 0.7 copy.36
  (34 shorter events, 0.9 us)
Async XLA Ops:
  10.7 155.6 %copy-start.6 = (f32[32,2]{0,1:T(2,128)S(1)}, f32[32,2]{0,1:T(2,128)}, u32[]{:S(2)}) copy-start(f32[32,2]{0,1:T(2,128)} %param.12) | copy-start | bytes 772
  10.7 156.4 %copy-start.4 = (bf16[4,27,16,16]{1,3,2,0:T(8,128)(2,1)S(1)}, bf16[4,27,16,16]{1,3,2,0:T(8,128)(2,1)}, u32[]{:S(2)}) copy-start(bf16[4,27,16,16]{1,3,2,0:T(8,128)(2,1)} %param.13) | copy-start | bytes 165892
  168.0 0.9 copy-start
  168.0 1.8 copy-start.5
  168.9 1.9 copy-start.1
  169.8 1.0 copy-start.3
  237.1 4.8 %copy-start.2 = (f32[2,128,384]{2,1,0:T(8,128)S(1)}, f32[2,128,384]{2,1,0:T(8,128)}, u32[]{:S(2)}) copy-start(f32[2,128,384]{2,1,0:T(8,128)} %get-tuple-element.21) | copy-start | bytes 1179652

commit v4 on v3

--- a/solution.py
+++ b/solution.py
@@ -18,16 +18,27 @@
     fine = fine.astype(jnp.float32) * unit
     coarse = coarse.astype(jnp.float32) * unit
     scale = 1.0 / math.sqrt(length)
-    fine_cos, fine_sin, coarse_cos, coarse_sin = lax.optimization_barrier(
-        (jnp.cos(fine), jnp.sin(fine), jnp.cos(coarse) * scale, jnp.sin(coarse) * scale)
+    return (
+        jnp.stack([jnp.cos(fine), jnp.sin(fine)]),
+        jnp.stack([jnp.cos(coarse), jnp.sin(coarse)]) * scale,
     )
-    fine_cos, fine_sin = fine_cos[None], fine_sin[None]
-    coarse_cos, coarse_sin = coarse_cos[:, None], coarse_sin[:, None]
-    table = jnp.stack([coarse_cos * fine_cos - coarse_sin * fine_sin, coarse_sin * fine_cos + coarse_cos * fine_sin])
-    return table.astype(jnp.bfloat16).reshape(2, length, length)
-
-
-def gradient_body(spaces, coils, estimate_ref, sens_ref, kdata_ref, mask_ref, par_ref, pe_ref, state_ref, out_ref, cells_ref,
+
+
+def fill_table(table, fine_ref, coarse_ref):
+    inner = fine_ref.shape[1]
+
+    @pl.loop(0, coarse_ref.shape[1])
+    def _(a):
+        cos, sin = coarse_ref[0, pl.ds(a, 1), :], coarse_ref[1, pl.ds(a, 1), :]
+        at = pl.ds(pl.multiple_of(a * inner, inner), inner)
+        table[0, at, :] = (cos * fine_ref[0] - sin * fine_ref[1]).astype(jnp.bfloat16)
+        table[1, at, :] = (sin * fine_ref[0] + cos * fine_ref[1]).astype(jnp.bfloat16)
+
+
+def gradient_body(spaces, coils, estimate_ref, mask_ref, par_fine, par_coarse, pe_fine, pe_coarse,
+                  sens_hbm, kdata_hbm, state_hbm, out_ref, cells_hbm,
+                  sens_ref, kdata_ref, state_ref, cells_ref, par_ref, pe_ref,
+                  sens_in, kdata_in, state_in, cells_out,
                   seen, whole, send_out, got_out, send_back, got_back, total, part, parts,
                   seen_sent, seen_got, out_sent, out_got, back_sent, back_got, part_sent, part_got):
     space = lax.axis_index("space")
@@ -39,6 +50,20 @@
     sites = positions * rows
     lines = positions * held
 
+    fetch_kdata = pltpu.make_async_copy(kdata_hbm, kdata_ref, kdata_in)
+    fetch_state = pltpu.make_async_copy(state_hbm, state_ref, state_in)
+    store_cells = pltpu.make_async_copy(cells_ref, cells_hbm, cells_out)
+
+    def fetch_sens(c):
+        return pltpu.make_async_copy(sens_hbm.at[:, c], sens_ref.at[:, c], sens_in.at[c])
+
+    @pl.loop(0, count)
+    def _(c):
+        fetch_sens(c).start()
+
+    fetch_state.start()
+    fetch_kdata.start()
+
     barrier = pltpu.get_barrier_semaphore()
 
     @pl.loop(1, spaces)
@@ -69,6 +94,7 @@
     for offset in range(1, coils):
         to_coil(estimate_ref, seen.at[coil], offset, seen_sent, seen_got).start()
     seen[coil] = estimate_ref[...]
+    fill_table(par_ref, par_fine, par_coarse)
     for offset in range(1, coils):
         to_coil(estimate_ref, seen.at[coil], offset, seen_sent, seen_got).wait()
     for part_of in range(2):
@@ -76,6 +102,7 @@
 
     @pl.loop(0, count)
     def _(c):
+        fetch_sens(c).wait()
         profile_real = sens_ref[0, c].reshape(sites, npar)
         profile_imag = sens_ref[1, c].reshape(sites, npar)
         real = profile_real * whole[0] - profile_imag * whole[1]
@@ -93,6 +120,8 @@
 
         got_out[c, space] = send_out[c, space]
 
+    fill_table(pe_ref, pe_fine, pe_coarse)
+    fetch_state.wait()
     half = state_ref.shape[0] // 2
     group = 16
 
@@ -103,6 +132,9 @@
             for position in range(positions):
                 cells = state_ref[side * half:(side + 1) * half, position, at, :].astype(f32)
                 cells_ref[side, at, position * half:(position + 1) * half, :] = jnp.swapaxes(cells, 0, 1).astype(bf16)
+
+    store_cells.start()
+    fetch_kdata.wait()
 
     @pl.loop(0, count)
     def _(c):
@@ -164,6 +196,7 @@
     for j in range(1, coils):
         result += parts[j].astype(f32)
     out_ref[...] = result
+    store_cells.wait()
 
     @pl.loop(0, count)
     def _(c):
@@ -179,6 +212,7 @@
     sites = positions * rows
     bf16, f32 = jnp.bfloat16, jnp.float32
     vmem = pl.BlockSpec(memory_space=pltpu.VMEM)
+    hbm = pl.BlockSpec(memory_space=pl.ANY)
     dma = pltpu.SemaphoreType.DMA
     message = pltpu.VMEM((count, spaces, held, 2 * sites), bf16)
     channels = state.shape[0]
@@ -188,9 +222,16 @@
             jax.ShapeDtypeStruct((2, sites, width), f32),
             jax.ShapeDtypeStruct((2, rows, positions * channels // 2, width), bf16),
         ),
-        in_specs=[vmem] * 7,
-        out_specs=(vmem, vmem),
+        in_specs=[vmem] * 6 + [hbm] * 3,
+        out_specs=(vmem, hbm),
         scratch_shapes=[
+            pltpu.VMEM(sens.shape, f32),
+            pltpu.VMEM(kdata.shape, f32),
+            pltpu.VMEM(state.shape, bf16),
+            pltpu.VMEM((2, rows, positions * channels // 2, width), bf16),
+            pltpu.VMEM((2, npar, npar), bf16),
+            pltpu.VMEM((2, npe, npe), bf16),
+            dma((count,)), dma, dma, dma,
             pltpu.VMEM((coils, 2, sites, width), bf16),
             pltpu.VMEM((2, sites, npar), f32),
             message, message, message, message,
@@ -202,7 +243,7 @@
         ],
         compiler_params=pltpu.CompilerParams(
             collective_id=0, has_side_effects=True, vmem_limit_bytes=60 * 1024 * 1024),
-    )(state[0:2].reshape(2, sites, width), sens, kdata, mask, dft_table(npar), dft_table(npe), state)
+    )(state[0:2].reshape(2, sites, width), mask, *dft_table(npar), *dft_table(npe), sens, kdata, state)
     return result.reshape(2, positions, rows, width), cells
 
 
@@ -375,10 +416,10 @@
     for layer in range(layers):
         source, target = layer % 2, 1 - layer % 2
 
-        @pl.loop(0, halves.shape[1] // (2 * unit))
+        @pl.loop(0, halves.shape[1] // (4 * unit))
         def _(pair, source=source):
-            for one in range(2):
-                index = 2 * pair + one
+            for one in range(4):
+                index = 4 * pair + one
                 at = pl.ds(pl.multiple_of(index * unit, unit), unit)
                 line = halves[source, at, :]
                 wide = line.astype(f32)
@@ -389,10 +430,9 @@
         left = halo_rows - 2 * layer - 2
         steps = -(-left // BLOCK)
 
-        @pl.loop(0, steps)
-        def _(index, layer=layer, target=target):
+        for index in range(steps):
             start = layer + index * BLOCK
-            inside = pl.ds(pl.multiple_of(start * 3 * unit, 3 * unit), (BLOCK + 2) * 3 * unit)
+            inside = pl.ds(start * 3 * unit, (BLOCK + 2) * 3 * unit)
             raw = jnp.dot(weight_ref[layer], shifted[inside, :], preferred_element_type=f32)
             hidden = jnp.maximum(raw + bias_ref[layer], 0.0)
             step = lax.broadcasted_iota(jnp.int32, (BLOCK * unit, 1), 0) // unit
@@ -400,7 +440,7 @@
             row_ok = jnp.where((row >= 0) & (row < total_rows), 1.0, 0.0)
             hidden = (hidden * (row_ok * column_ok)).astype(bf16)
             update = jnp.dot(mixer_ref[layer], hidden, preferred_element_type=f32)
-            at = pl.ds(pl.multiple_of((start + 1) * unit, unit), BLOCK * unit)
+            at = pl.ds((start + 1) * unit, BLOCK * unit)
             halves[target, at, :] = (halves[target, at, :].astype(f32) + update).astype(bf16)
 
     for half in range(2):

time: 246 us -> 225 us (0.915)
  Pallas kernels: 222 us -> 203 us
  other arithmetic: 8.56 us -> 4.92 us
    pallas_call x1, Pallas kernels: 66.3 us -> 53.7 us  [couple(): pl.pallas_call(functools.partial(couplings_body, layers, rows, width, lan...]
    pallas_call x1, Pallas kernels: 156 us -> 149 us  [find_gradient(): pl.pallas_call(functools.partial(gradient_body, spaces, coils), out_shape...]
    another operation x4 -> x2, other arithmetic: 6.06 us -> 1.42 us  [dft_table(): jnp.stack([jnp.cos(fine), jnp.sin(fine)])]
where the time goes in v4:
time: 225 us; the launch traced here: 221 us
  Pallas kernels  203 us (90%)
  local copies, waits for them, and re-layouts  12.7 us (6%)
  other arithmetic  4.92 us (2%)
    pallas_call x1, Pallas kernels, find_gradient(): pl.pallas_call(functools.partial(gradient_body, spaces, coils), out_shape...  149 us
    pallas_call x1, Pallas kernels, couple(): pl.pallas_call(functools.partial(couplings_body, layers, rows, width, lan...  53.7 us
    transpose x1, local copies, waits for them, and re-layouts, couple(): jnp.transpose(out, (0, 3, 2, 1, 4))  4.75 us

profile of v4, /device:TPU:15, one launch (start us, length us, event | category | flops | bytes accessed | tf_op | source)
XLA Modules:
  0.0 221.0 jit_solution(13567766269238127482)
XLA Ops:
  0.6 0.8 reshape.346
  1.4 0.7 tile.18
  2.1 0.7 tile.20.inject_ref
  2.8 0.4 fusion.24
  3.2 0.7 maximum_multiply_fusion.1.par_coarse
  3.9 1.6 slice.40
  5.5 0.4 fusion.16
  5.9 0.7 pad_maximum_fusion.1.par_fine
  6.6 0.6 fusion.29
  7.2 0.7 maximum_multiply_fusion.pe_coarse
  7.9 0.5 fusion.26
  8.5 0.7 pad_maximum_fusion.pe_fine
  9.2 1.0 tile.21.bias_ref
  11.0 0.9 copy.15
  12.0 0.2 maximum_maximum_fusion
  12.2 0.1 concatenate.21
  12.4 0.1 pad_dynamic-update-slice_fusion.4
  12.5 0.1 pad_dynamic-update-slice_fusion.3
  12.6 0.1 pad_dynamic-update-slice_fusion.2
  12.7 0.1 pad_dynamic-update-slice_fusion.weight_ref
  12.9 149.0 %shard_map.95 = (f32[2,128,384]{2,1,0:T(8,128)}, bf16[2,64,32,384]{3,2,1,0:T(8,128)(2,1)}) custom-call(bf16[2,128,384]{2,1,0:T(8,128)(2,1)} %bitcast.39, s32[48,1024]{1,0:T(8,128)} %mask_ref.1, f32[2,32,768]{2,1,0:T(8,128)} %pad_maximum_fusion.1.par_fine, f32[2,24,768]{2,1,0:T(8,128)} %maximum_multiply_fusion.1.par_coarse, ...), custom_call_target="tpu_custom_call" | custom-call | tf_op jit(solution)/shard_map/pallas_call | solution.py:219
  161.8 53.7 %shard_map.96 = bf16[2,2048,384]{2,1,0:T(8,128)(2,1)} custom-call(bf16[2,64,32,384]{3,2,1,0:T(8,128)(2,1)} %get-tuple-element.4.cells_ref, f32[2,2,64,384]{3,2,1,0:T(8,128)} %bitcast.37, f32[2,2,32,1]{3,2,1,0:T(8,128)} %tile.20.inject_ref, bf16[4,192,768]{2,1,0:T(8,128)(2,1)} %copy-done.1, bf16[4,192,192]{2,1,0:T(8,128)(2,1)} %copy-done.3, ...), custom_call_target="tpu_custom_call" | custom-call | tf_op jit(solution)/shard_map/pallas_call | solution.py:462
  215.5 4.7 %copy.18 = bf16[2,16,2,64,384]{4,3,2,1,0:T(8,128)(2,1)} copy(bf16[2,16,2,64,384]{4,1,2,3,0:T(8,128)(2,1)} %bitcast.34) | data formatting | bytes 6291456 | tf_op jit(solution)/shard_map/transpose | solution.py:478
  220.3 0.7 copy.36
  (30 shorter events, 1.0 us)
Async XLA Ops:
  5.9 4.3 %copy-start = (bf16[4,16,16]{2,1,0:T(8,128)(2,1)S(1)}, bf16[4,16,16]{2,1,0:T(8,128)(2,1)}, u32[]{:S(2)}) copy-start(bf16[4,16,16]{2,1,0:T(8,128)(2,1)} %param.15) | copy-start | bytes 6148
  7.2 3.9 %copy-start.4 = (bf16[4,27,16,16]{1,3,2,0:T(8,128)(2,1)S(1)}, bf16[4,27,16,16]{1,3,2,0:T(8,128)(2,1)}, u32[]{:S(2)}) copy-start(bf16[4,27,16,16]{1,3,2,0:T(8,128)(2,1)} %param.13) | copy-start | bytes 165892
  11.0 1.1 copy-start.3
  12.8 149.0 %copy-start.1 = (bf16[4,192,768]{2,1,0:T(8,128)(2,1)}, bf16[4,192,768]{2,1,0:T(8,128)(2,1)S(1)}, u32[]{:S(2)}) copy-start(bf16[4,192,768]{2,1,0:T(8,128)(2,1)S(1)} %pad_dynamic-update-slice_fusion.weight_ref) | copy-start | bytes 3538948
  215.5 4.8 %copy-start.2 = (f32[2,128,384]{2,1,0:T(8,128)S(1)}, f32[2,128,384]{2,1,0:T(8,128)}, u32[]{:S(2)}) copy-start(f32[2,128,384]{2,1,0:T(8,128)} %get-tuple-element.5) | copy-start | bytes 1179652

commit v5 on v4

--- a/solution.py
+++ b/solution.py
@@ -3,6 +3,7 @@
 
 import jax
 import jax.numpy as jnp
+import numpy as np
 from jax import lax
 from jax.experimental import pallas as pl
 from jax.experimental.pallas import tpu as pltpu
@@ -11,16 +12,13 @@
 
 def dft_table(length):
     inner = 32
-    column = lax.iota(jnp.int32, length)[None, :]
-    fine = lax.iota(jnp.int32, inner)[:, None] * column % length
-    coarse = (lax.iota(jnp.int32, length // inner)[:, None] * inner) * column % length
-    unit = 2.0 * math.pi / length
-    fine = fine.astype(jnp.float32) * unit
-    coarse = coarse.astype(jnp.float32) * unit
+    column = np.arange(length)[None, :]
+    fine = np.arange(inner)[:, None] * column % length * (2.0 * math.pi / length)
+    coarse = np.arange(0, length, inner)[:, None] * column % length * (2.0 * math.pi / length)
     scale = 1.0 / math.sqrt(length)
     return (
-        jnp.stack([jnp.cos(fine), jnp.sin(fine)]),
-        jnp.stack([jnp.cos(coarse), jnp.sin(coarse)]) * scale,
+        jnp.asarray(np.stack([np.cos(fine), np.sin(fine)]).astype(np.float32)),
+        jnp.asarray((np.stack([np.cos(coarse), np.sin(coarse)]) * scale).astype(np.float32)),
     )
 
 

time: 225 us -> 224 us (level)
  other arithmetic: 4.92 us -> 0.17 us
  local copies, waits for them, and re-layouts: 12.7 us -> 16.3 us
    unnamed x28, local copies, waits for them, and re-layouts: 2.75 us -> 6.33 us
where the time goes in v5:
time: 224 us; the launch traced here: 220 us
  Pallas kernels  203 us (91%)
  local copies, waits for them, and re-layouts  16.3 us (7%)
    pallas_call x1, Pallas kernels, find_gradient(): pl.pallas_call(functools.partial(gradient_body, spaces, coils), out_shape...  149 us
    pallas_call x1, Pallas kernels, couple(): pl.pallas_call(functools.partial(couplings_body, layers, rows, width, lan...  53.7 us
    unnamed x28, local copies, waits for them, and re-layouts  6.33 us
    transpose x1, local copies, waits for them, and re-layouts, couple(): jnp.transpose(out, (0, 3, 2, 1, 4))  4.75 us

profile of v5, /device:TPU:15, one launch (start us, length us, event | category | flops | bytes accessed | tf_op | source)
XLA Modules:
  0.0 219.8 jit_solution(14850688182335541316)
XLA Ops:
  0.7 0.8 reshape.36
  1.5 0.7 tile.18
  2.2 0.7 tile.20.inject_ref
  2.9 1.6 slice.40
  4.5 1.0 tile.21.bias_ref
  5.5 0.7 constant_dynamic-update-slice_fusion.11
  6.2 0.8 constant_dynamic-update-slice_fusion.10
  7.0 0.8 constant_dynamic-update-slice_fusion.9
  7.8 0.8 constant_dynamic-update-slice_fusion.8
  8.6 0.8 constant_dynamic-update-slice_fusion.7
  9.4 0.1 constant_dynamic-update-slice_fusion.6
  9.5 0.1 constant_dynamic-update-slice_fusion.5
  9.5 0.1 constant_dynamic-update-slice_fusion.4
  9.9 0.9 copy.19
  10.8 0.2 maximum_maximum_fusion
  11.0 0.1 concatenate.21
  11.2 0.1 pad_dynamic-update-slice_fusion.4
  11.3 0.1 pad_dynamic-update-slice_fusion.3
  11.4 0.1 pad_dynamic-update-slice_fusion.2
  11.6 0.1 pad_dynamic-update-slice_fusion.weight_ref
  11.7 149.0 %shard_map.131 = (f32[2,128,384]{2,1,0:T(8,128)}, bf16[2,64,32,384]{3,2,1,0:T(8,128)(2,1)}) custom-call(bf16[2,128,384]{2,1,0:T(8,128)(2,1)} %bitcast.39, s32[48,1024]{1,0:T(8,128)} %mask_ref.1, f32[2,32,768]{2,1,0:T(8,128)} %constant.11.clone.par_fine, f32[2,24,768]{2,1,0:T(8,128)} %constant.12.clone.par_coarse, f32[2,32,1024]{2,1,0:T(8,128)} %constant.13.clone.pe_fine, ...), custom_call_target="tpu_custom_call" | custom-call | tf_op jit(solution)/shard_map/pallas_call | solution.py:217
  160.7 53.7 %shard_map.132 = bf16[2,2048,384]{2,1,0:T(8,128)(2,1)} custom-call(bf16[2,64,32,384]{3,2,1,0:T(8,128)(2,1)} %get-tuple-element.4.cells_ref, f32[2,2,64,384]{3,2,1,0:T(8,128)} %bitcast.37, f32[2,2,32,1]{3,2,1,0:T(8,128)} %tile.20.inject_ref, bf16[4,192,768]{2,1,0:T(8,128)(2,1)} %copy-done.1, bf16[4,192,192]{2,1,0:T(8,128)(2,1)} %copy-done.3, ...), custom_call_target="tpu_custom_call" | custom-call | tf_op jit(solution)/shard_map/pallas_call | solution.py:460
  214.4 4.7 %copy.22 = bf16[2,16,2,64,384]{4,3,2,1,0:T(8,128)(2,1)} copy(bf16[2,16,2,64,384]{4,1,2,3,0:T(8,128)(2,1)} %bitcast.34) | data formatting | bytes 6291456 | tf_op jit(solution)/shard_map/transpose | solution.py:476
  219.1 0.7 copy.40
  (20 shorter events, 0.4 us)
Async XLA Ops:
  0.6 8.7 %copy-start = (bf16[4,16,16]{2,1,0:T(8,128)(2,1)S(1)}, bf16[4,16,16]{2,1,0:T(8,128)(2,1)}, u32[]{:S(2)}) copy-start(bf16[4,16,16]{2,1,0:T(8,128)(2,1)} %param.19) | copy-start | bytes 6148
  0.6 9.2 %copy-start.4 = (bf16[4,27,16,16]{1,3,2,0:T(8,128)(2,1)S(1)}, bf16[4,27,16,16]{1,3,2,0:T(8,128)(2,1)}, u32[]{:S(2)}) copy-start(bf16[4,27,16,16]{1,3,2,0:T(8,128)(2,1)} %param.17) | copy-start | bytes 165892
  9.9 1.1 copy-start.3
  11.7 149.0 %copy-start.1 = (bf16[4,192,768]{2,1,0:T(8,128)(2,1)}, bf16[4,192,768]{2,1,0:T(8,128)(2,1)S(1)}, u32[]{:S(2)}) copy-start(bf16[4,192,768]{2,1,0:T(8,128)(2,1)S(1)} %pad_dynamic-update-slice_fusion.weight_ref) | copy-start | bytes 3538948
  214.3 4.8 %copy-start.2 = (f32[2,128,384]{2,1,0:T(8,128)S(1)}, f32[2,128,384]{2,1,0:T(8,128)}, u32[]{:S(2)}) copy-start(f32[2,128,384]{2,1,0:T(8,128)} %get-tuple-element.5) | copy-start | bytes 1179652
